TPU v7x, 256 devices: a whole 4x4x8 slice. The times are simulated.
256 devices in a mesh: pipe: 4 (over x), dp: 64 (over z, y, core).
Axes of the slice: x: 4, y: 4, z: 8, core: 2. Of those that a mesh axis runs over, the one named last changes fastest.
Arguments:
- hidden: bfloat16 [4, 2048, 3072], P(None, 'dp'), may hold values from -6 to 6
- w_query: bfloat16 [4, 2, 3072, 1536], P('pipe', None, 'dp'), may hold values from -0.109375 to 0.109375
- w_key: bfloat16 [4, 2, 3072, 1536], P('pipe', None, 'dp'), may hold values from -0.109375 to 0.109375
- w_value: bfloat16 [4, 2, 3072, 1536], P('pipe', None, 'dp'), may hold values from -0.109375 to 0.109375
- w_out: bfloat16 [4, 2, 1536, 3072], P('pipe', None, None, 'dp'), may hold values from -0.15625 to 0.15625
- video_len: int32 [4, 16], replicated, may hold values from 1 to 96
- audio_len: int32 [4, 16], replicated, may hold values from 1 to 32
Outputs:
- final: bfloat16 [4, 2048, 3072], P('pipe', 'dp')
All inputs are finite; a program needn't handle non-finite values.
Results may differ from a plain program's by a relative error of at most 0.017.
Values may be sent and summed in bfloat16 or wider, within the bound.
No kernel may reach another device: no remote copies, remote signals or barrier semaphores. Data moves between devices by JAX's collectives and lax.ppermute only.
A program may use at most 128 MiB of HBM per device.

v0:
```python
import functools

import jax
import jax.numpy as jnp
from jax import lax
from jax.experimental import pallas as pl
from jax.experimental.pallas import tpu as pltpu
from jax.sharding import Mesh
from jax.sharding import PartitionSpec as P

HEAD = 128
NEAR = [(0, 1), (1, 0), (2, 3), (3, 2)]
FAR = [(1, 2), (2, 1), (3, 0), (0, 3)]
SWAP = [(0, 1), (1, 0)]


def rms_norm(values):
    wide = values.astype(jnp.float32)
    scale = lax.rsqrt(jnp.mean(wide * wide, axis=-1, keepdims=True) + 1e-06)
    return (wide * scale).astype(jnp.bfloat16)


def near(value):
    return lax.ppermute(value, "y", NEAR)


def far(value):
    return lax.ppermute(value, "y", FAR)


def swap(value):
    return lax.ppermute(value, "core", SWAP)


def up(value):
    return lax.ppermute(value, "z", [(place, (place + 1) % 8) for place in range(8)])


def down(value):
    return lax.ppermute(value, "z", [(place, (place - 1) % 8) for place in range(8)])


def beside(value):
    return lax.ppermute(value, "pipe", NEAR)


def around(value):
    return lax.ppermute(value, "pipe", FAR)


SHALLOW = (256, 0, 128, 256)
OFFSETS = (0, 7, 6, 5, 1, 2, 3, 4)


def block_kernel(ctl, *refs, tokens, shallow, pieces):
    mine, by_near, by_far, cross, swapped, swapped_cross = refs[:6]
    weights = refs[6 : 6 + pieces]
    keep, give, held, normed, sums, mixed_all, sems = refs[6 + pieces :]
    size = sums.shape[2]
    places = []
    if shallow:
        rows = pl.ds(0, shallow)
        places += [held.at[:, slot, rows] for slot in range(7)]
        places += [held.at[0:2, 7, rows], held.at[2:4, 7, rows]]
    if shallow < size:
        rows = pl.ds(shallow, size - shallow)
        places += [held.at[index // 2, pl.ds(index % 2 * 4, 4), rows] for index in range(8)]
    copies = [
        pltpu.make_async_copy(weights[index], place, sems.at[index])
        for index, place in enumerate(places)
    ]
    for copy in copies:
        copy.start()
    flip, core, section, depth = ctl[0], ctl[1], ctl[4], ctl[5]

    def columns(slot):
        place = (depth + ctl[8 + slot]) & 7
        return pl.ds(pl.multiple_of(place * size, 128), size)

    for slot in range(8):
        cols, to = columns(slot), pl.ds(slot * size, size)
        for block, (own, other) in enumerate(
            ((mine, swapped.at[0]), (by_near, swapped.at[1]), (cross, swapped_cross), (by_far, swapped.at[2]))
        ):
            normed[pl.ds(2 * block * tokens, tokens), to] = own[:, cols]
            normed[pl.ds((2 * block + 1) * tokens, tokens), to] = other[:, cols]

    for copy in copies:
        copy.wait()
    for index in range(4):
        array = section ^ index

        @pl.when(array != 3)
        def _():
            sums[array] = jnp.dot(
                normed[...],
                held[index].reshape(8 * size, size),
                preferred_element_type=jnp.float32,
            )

    rows = 4 * tokens
    heads = size // HEAD
    key_place = lax.broadcasted_iota(jnp.int32, (rows, rows), 1) ^ flip
    query_place = lax.broadcasted_iota(jnp.int32, (rows, HEAD), 0) ^ flip
    video = 3 * tokens
    first = jnp.where(core == 0, video, 0)
    own_low = jnp.where(core == 0, 0, video)
    own_high = jnp.where(core == 0, video, rows)
    live = (query_place >= own_low) & (query_place < own_high)
    for sample in range(2):
        valid = (key_place >= first) & (key_place < first + ctl[2 + sample])
        span = pl.ds(sample * rows, rows)
        spans = [pl.ds(head * HEAD, HEAD) for head in range(heads)]
        scores = [
            lax.dot_general(
                (sums[0, span, cols] * HEAD ** (-0.5)).astype(jnp.bfloat16),
                sums[1, span, cols].astype(jnp.bfloat16),
                (((1,), (1,)), ((), ())),
                preferred_element_type=jnp.float32,
            )
            for cols in spans
        ]
        scores = [jnp.where(valid, score, -1e30) for score in scores]
        powers = [jnp.exp(score - jnp.max(score, axis=-1, keepdims=True)) for score in scores]
        shares = [
            (power * (1.0 / jnp.sum(power, axis=-1, keepdims=True))).astype(jnp.bfloat16)
            for power in powers
        ]
        mixed = [
            jnp.dot(share, sums[2, span, cols].astype(jnp.bfloat16), preferred_element_type=jnp.float32)
            for share, cols in zip(shares, spans)
        ]
        for head, cols in enumerate(spans):
            mixed_all[span, cols] = jnp.where(live, mixed[head], 0.0).astype(jnp.bfloat16)
    last = section ^ 3

    def project(piece, slot):
        made = lax.dot_general(
            mixed_all[...], piece, (((1,), (1,)), ((), ())), preferred_element_type=jnp.float32
        ).astype(jnp.bfloat16)
        for block in range(4):
            keep[block, :, columns(slot)] = made[2 * block * tokens : (2 * block + 1) * tokens]
            give[block, :, columns(slot)] = made[(2 * block + 1) * tokens : (2 * block + 2) * tokens]

    @pl.loop(0, 8)
    def _(slot):
        project(held[last, slot], slot)


def run_block(ctl, blocks, weights, tokens, width, shallow):
    size = weights[0].shape[2]
    vmem = pl.BlockSpec(memory_space=pltpu.VMEM)
    out = jax.ShapeDtypeStruct((4, tokens, width), jnp.bfloat16)
    count = 8 * tokens
    there = pl.BlockSpec(memory_space=pltpu.HBM)
    return pl.pallas_call(
        functools.partial(
            block_kernel, tokens=tokens, shallow=shallow, pieces=len(weights)
        ),
        out_shape=(out, out),
        in_specs=[pl.BlockSpec(memory_space=pltpu.SMEM)] + [vmem] * 6 + [there] * len(weights),
        out_specs=(vmem, vmem),
        scratch_shapes=[
            pltpu.VMEM((4, 8, size, size), jnp.bfloat16),
            pltpu.VMEM((count, width), jnp.bfloat16),
            pltpu.VMEM((3, count, size), jnp.float32),
            pltpu.VMEM((count, size), jnp.bfloat16),
            pltpu.SemaphoreType.DMA((17,)),
        ],
        compiler_params=pltpu.CompilerParams(vmem_limit_bytes=24 << 20),
        cost_estimate=pl.CostEstimate(
            flops=8 * count * width * size,
            bytes_accessed=8 * width * size + 6 * count * width,
            transcendentals=count * size,
        ),
    )(ctl, *blocks, *weights)


def pack_kernel(query, key, value, out, packed):
    quarter = packed.shape[4]
    for tower in range(2):
        for part in range(4):
            cols = pl.ds(part * quarter, quarter)
            packed[0, part, tower] = query[tower, :, cols]
            packed[1, part, tower] = key[tower, :, cols]
            packed[2, part, tower] = value[tower, :, cols]
            packed[3, part, tower] = out[tower, cols, :].T


def pack(query, key, value, out):
    towers, rows, features = query.shape
    vmem = pl.BlockSpec(memory_space=pltpu.VMEM)
    return pl.pallas_call(
        pack_kernel,
        out_shape=jax.ShapeDtypeStruct((4, 4, towers, rows, features // 4), jnp.bfloat16),
        in_specs=[vmem] * 4,
        out_specs=vmem,
    )(query, key, value, out)


def gather_tokens(mine):
    half = mine.shape[0] // 2
    by_near, by_far = near(mine), far(mine)
    pair = swap(jnp.stack([mine, by_near, by_far]))
    cross = jnp.concatenate([near(by_far[:half]), far(by_near[half:])])
    return mine, by_near, by_far, cross, pair, swap(cross)


def reduce_tokens(state, keep, give):
    half = state.shape[0] // 2
    total = keep + swap(give)
    low = near(total[2, :half]).astype(jnp.float32)
    high = far(total[2, half:]).astype(jnp.float32)
    to_far = jnp.concatenate(
        [(total[3, :half].astype(jnp.float32) + low).astype(jnp.bfloat16), total[3, half:]]
    )
    to_near = jnp.concatenate(
        [total[1, :half], (total[1, half:].astype(jnp.float32) + high).astype(jnp.bfloat16)]
    )
    by_near, by_far = near(to_near), far(to_far)
    update = total[0].astype(jnp.float32) + by_near.astype(jnp.float32) + by_far.astype(jnp.float32)
    return (state.astype(jnp.float32) + update).astype(jnp.bfloat16)


def across(shard):
    by_beside, by_around = beside(shard), around(shard)
    return jnp.stack([shard, by_beside, beside(by_around), by_around])


def deep(block):
    below = [up(block)]
    above = [down(block)]
    for _ in range(2):
        below.append(up(below[-1]))
        above.append(down(above[-1]))
    return below, above


def finish_deep(four):
    below, above = deep(four)
    return [four, *below, *above, up(below[-1][:2]), down(above[-1][2:])]


def finish_across(lower, upper):
    by_beside = beside(lower), beside(upper)
    by_around = around(lower), around(upper)
    crossed = beside(by_around[0]), around(by_beside[1])
    return [lower, upper, *by_beside, *crossed, *by_around]


def spread(shards):
    zero, one, two, three = shards
    cut = SHALLOW
    size = zero.shape[0]
    shallow = [finish_deep(across(zero[: cut[0]])), []]
    both = across(jnp.concatenate([two[: cut[2]], three[: cut[3]]]))
    shallow.append(finish_deep(both[:, : cut[2]]))
    shallow.append(finish_deep(both[:, cut[2] :]))
    rest = zero[cut[0] :]
    below, above = deep(rest)
    lower = jnp.stack([rest, *below])
    upper = jnp.stack([*above, up(below[-1])])
    across_all = [finish_across(lower, upper)]
    rest = jnp.concatenate([one, two[cut[2] :], three[cut[3] :]])
    below, above = deep(rest)
    ends = up(below[-1][:size]), down(above[-1][size:])
    start = 0
    for layer in (1, 2, 3):
        stop = start + size - cut[layer]
        end = ends[0] if layer == 1 else ends[1][start - size : stop - size]
        lower = jnp.stack([part[start:stop] for part in [rest, *below]])
        upper = jnp.stack([part[start:stop] for part in above] + [end])
        across_all.append(finish_across(lower, upper))
        start = stop
    return [early + late for early, late in zip(shallow, across_all)]


def section(hidden, w_query, w_key, w_value, w_out, video_len, audio_len):
    batch = lax.axis_index("pipe")
    depth = lax.axis_index("z")
    ring = lax.axis_index("y")
    core = lax.axis_index("core")
    _, tokens, width = hidden.shape
    features = w_query.shape[3]
    rows = w_query.shape[2]
    quarter = features // 4
    layers = 4
    parts = pack(w_query[0], w_key[0], w_value[0], w_out[0]).reshape(32, rows, quarter)
    moved = lax.all_to_all(parts, ("pipe", "y", "core"), 0, 0, tiled=True)
    moved = moved.reshape(layers, 8 * rows, quarter)
    gathered = spread(moved)
    state = lax.dynamic_index_in_dim(hidden, batch, 0, keepdims=False)
    low, high = ring % 2, ring // 2
    lengths = jnp.where(core == 0, audio_len[batch], video_len[batch])
    flip = 2 * tokens * low + tokens * core
    zero = jnp.int32(0)
    ctl = jnp.stack(
        [flip, core, lengths[2 * depth + high], lengths[2 * depth + 1 - high], batch, depth, zero, zero]
        + [jnp.int32(offset) for offset in OFFSETS]
    ).astype(jnp.int32)
    for layer in range(layers):
        blocks = gather_tokens(rms_norm(state))
        keep, give = run_block(ctl, blocks, gathered[layer], tokens, width, SHALLOW[layer])
        state = reduce_tokens(state, keep, give)
    return state[None]


def solution(mesh):
    inner = Mesh(mesh.devices.reshape(4, 8, 4, 2), ("pipe", "z", "y", "core"))
    dp = ("z", "y", "core")
    return jax.shard_map(
        section,
        mesh=inner,
        in_specs=(
            P(None, dp, None),
            P("pipe", None, dp, None),
            P("pipe", None, dp, None),
            P("pipe", None, dp, None),
            P("pipe", None, None, dp),
            P(),
            P(),
        ),
        out_specs=P("pipe", dp, None),
        check_vma=False,
    )
```

profile of v0, /device:TPU:6, one launch (start us, length us, event | category | flops | bytes accessed | tf_op | source)
XLA Modules:
  0.0 490.0 jit_solution(12783387820083063057)
XLA Ops:
  4.8 7.7 %all-to-all-start = ((bf16[32,48,384]{2,1,0:T(8,128)(2,1)}), bf16[32,48,384]{2,1,0:T(8,128)(2,1)S(1)}, u32[]{:S(2)}, u32[]{:S(2)}) async-start(bf16[32,48,384]{2,1,0:T(8,128)(2,1)} %bitcast.214), calls=%async_computation | async-start | bytes 2359296 | tf_op jit(solution)/shard_map/all_to_all | solution.py:289
  12.7 16.5 %all-to-all-done = bf16[32,48,384]{2,1,0:T(8,128)(2,1)S(1)} async-done(((bf16[32,48,384]{2,1,0:T(8,128)(2,1)}), bf16[32,48,384]{2,1,0:T(8,128)(2,1)S(1)}, u32[]{:S(2)}, u32[]{:S(2)}) %all-to-all-start) | async-done | bytes 1179680 | tf_op jit(solution)/shard_map/all_to_all | solution.py:289
  45.9 4.0 collective-permute-start.12
  52.1 4.5 collective-permute-done.3
  56.7 9.6 %collective-permute-done.9.refs_7_ = bf16[4,256,384]{2,1,0:T(8,128)(2,1)S(1)} collective-permute-done((bf16[4,256,384]{2,1,0:T(8,128)(2,1)S(1)}, bf16[4,256,384]{2,1,0:T(8,128)(2,1)S(1)}, u32[]{:S(2)}, u32[]{:S(2)}) %collective-permute-start.9) | collective-permute-done | bytes 786464 | tf_op jit(solution)/shard_map/ppermute | solution.py:36
  75.9 11.4 %collective-permute-done.17 = bf16[128,384]{1,0:T(8,128)(2,1)S(1)} collective-permute-done((bf16[128,384]{1,0:T(8,128)(2,1)S(1)}, bf16[128,384]{1,0:T(8,128)(2,1)S(1)}, u32[]{:S(2)}, u32[]{:S(2)}) %collective-permute-start.17) | collective-permute-done | bytes 98336 | tf_op jit(solution)/shard_map/ppermute | solution.py:36
  89.3 4.2 collective-permute-done.18
  107.2 25.4 %collective-permute-done.23 = bf16[128,384]{1,0:T(8,128)(2,1)S(1)} collective-permute-done((bf16[128,384]{1,0:T(8,128)(2,1)S(1)}, bf16[128,384]{1,0:T(8,128)(2,1)S(1)}, u32[]{:S(2)}, u32[]{:S(2)}) %collective-permute-start.23) | collective-permute-done | bytes 98336 | tf_op jit(solution)/shard_map/ppermute | solution.py:36
  136.8 7.2 %collective-permute-done.26.refs_21_ = bf16[4,128,384]{2,1,0:T(8,128)(2,1)} collective-permute-done((bf16[4,128,384]{2,1,0:T(8,128)(2,1)S(1)}, bf16[4,128,384]{2,1,0:T(8,128)(2,1)}, u32[]{:S(2)}, u32[]{:S(2)}) %collective-permute-start.26) | collective-permute-done | bytes 393248 | tf_op jit(solution)/shard_map/ppermute | solution.py:48
  151.1 8.4 %collective-permute-done.67 = bf16[384,384]{1,0:T(8,128)(2,1)} collective-permute-done((bf16[384,384]{1,0:T(8,128)(2,1)}, bf16[384,384]{1,0:T(8,128)(2,1)}, u32[]{:S(2)}, u32[]{:S(2)}) %collective-permute-start.67) | collective-permute-done | bytes 294944 | tf_op jit(solution)/shard_map/ppermute | solution.py:44
  169.7 7.4 %collective-permute-done.42 = bf16[768,384]{1,0:T(8,128)(2,1)S(1)} collective-permute-done((bf16[768,384]{1,0:T(8,128)(2,1)}, bf16[768,384]{1,0:T(8,128)(2,1)S(1)}, u32[]{:S(2)}, u32[]{:S(2)}) %collective-permute-start.42) | collective-permute-done | bytes 589856 | tf_op jit(solution)/shard_map/ppermute | solution.py:36
  177.1 7.5 %collective-permute-done.15.refs_13_ = bf16[2,256,384]{2,1,0:T(8,128)(2,1)S(1)} collective-permute-done((bf16[2,256,384]{2,1,0:T(8,128)(2,1)S(1)}, bf16[2,256,384]{2,1,0:T(8,128)(2,1)S(1)}, u32[]{:S(2)}, u32[]{:S(2)}) %collective-permute-start.15) | collective-permute-done | bytes 393248 | tf_op jit(solution)/shard_map/ppermute | solution.py:36
  184.7 9.1 %shard_map.74 = (bf16[4,32,3072]{2,1,0:T(8,128)(2,1)S(1)}, bf16[4,32,3072]{2,1,0:T(8,128)(2,1)S(1)}) custom-call(s32[16]{0:T(128)S(1)} %stack.212.ctl, bf16[32,3072]{1,0:T(8,128)(2,1)S(1)} %copy-done.1, bf16[32,3072]{1,0:T(8,128)(2,1)S(1)} %collective-permute-done.refs_1_, bf16[32,3072]{1,0:T(8,128)(2,1)S(1)} %collective-permute-done.1.refs_2_, ...), custom_call_target="tpu_custom_call" | custom-call | flops 2415919104 | bytes 14155776 | tf_op jit(solution)/shard_map/pallas_call | solution.py:156
  205.2 4.5 collective-permute-done.46
  212.5 4.9 collective-permute-done.34
  219.8 5.9 %collective-permute-done.36.refs_2_ = bf16[32,3072]{1,0:T(8,128)(2,1)S(1)} collective-permute-done((bf16[32,3072]{1,0:T(8,128)(2,1)S(1)}, bf16[32,3072]{1,0:T(8,128)(2,1)S(1)}, u32[]{:S(2)}, u32[]{:S(2)}) %collective-permute-start.36) | collective-permute-done | bytes 196640 | tf_op jit(solution)/shard_map/ppermute | solution.py:28
  229.0 5.6 %collective-permute-done.71.refs_10_ = bf16[4,128,384]{2,1,0:T(8,128)(2,1)S(1)} collective-permute-done((bf16[4,128,384]{2,1,0:T(8,128)(2,1)S(1)}, bf16[4,128,384]{2,1,0:T(8,128)(2,1)S(1)}, u32[]{:S(2)}, u32[]{:S(2)}) %collective-permute-start.71) | collective-permute-done | bytes 393248 | tf_op jit(solution)/shard_map/ppermute | solution.py:40
  243.5 5.1 %collective-permute-done.38 = bf16[16,3072]{1,0:T(8,128)(2,1)S(1)} collective-permute-done((bf16[16,3072]{1,0:T(8,128)(2,1)S(1)}, bf16[16,3072]{1,0:T(8,128)(2,1)S(1)}, u32[]{:S(2)}, u32[]{:S(2)}) %collective-permute-start.38) | collective-permute-done | bytes 98336 | tf_op jit(solution)/shard_map/ppermute | solution.py:28
  248.7 16.4 %collective-permute-done.48.refs_8_ = bf16[4,384,384]{2,1,0:T(8,128)(2,1)S(1)} collective-permute-done((bf16[4,384,384]{2,1,0:T(8,128)(2,1)S(1)}, bf16[4,384,384]{2,1,0:T(8,128)(2,1)S(1)}, u32[]{:S(2)}, u32[]{:S(2)}) %collective-permute-start.48) | collective-permute-done | bytes 1179680 | tf_op jit(solution)/shard_map/ppermute | solution.py:44
  265.3 23.5 %collective-permute-done.51.refs_10_ = bf16[4,384,384]{2,1,0:T(8,128)(2,1)S(1)} collective-permute-done((bf16[4,384,384]{2,1,0:T(8,128)(2,1)S(1)}, bf16[4,384,384]{2,1,0:T(8,128)(2,1)S(1)}, u32[]{:S(2)}, u32[]{:S(2)}) %collective-permute-start.51) | collective-permute-done | bytes 1179680 | tf_op jit(solution)/shard_map/ppermute | solution.py:44
  290.6 9.3 %shard_map.75 = (bf16[4,32,3072]{2,1,0:T(8,128)(2,1)S(1)}, bf16[4,32,3072]{2,1,0:T(8,128)(2,1)S(1)}) custom-call(s32[16]{0:T(128)S(1)} %stack.212.ctl, bf16[32,3072]{1,0:T(8,128)(2,1)S(1)} %fusion.8.refs_0_, bf16[32,3072]{1,0:T(8,128)(2,1)S(1)} %collective-permute-done.35.refs_1_, bf16[32,3072]{1,0:T(8,128)(2,1)S(1)} %collective-permute-done.36.refs_2_, ...), custom_call_target="tpu_custom_call" | custom-call | flops 2415919104 | bytes 14155776 | tf_op jit(solution)/shard_map/pallas_call | solution.py:156
  312.9 5.6 %collective-permute-done.76 = bf16[384,384]{1,0:T(8,128)(2,1)S(1)} collective-permute-done((bf16[384,384]{1,0:T(8,128)(2,1)S(1)}, bf16[384,384]{1,0:T(8,128)(2,1)S(1)}, u32[]{:S(2)}, u32[]{:S(2)}) %collective-permute-start.76) | collective-permute-done | bytes 294944 | tf_op jit(solution)/shard_map/ppermute | solution.py:40
  320.8 5.1 %collective-permute-done.58 = bf16[32,3072]{1,0:T(8,128)(2,1)S(1)} collective-permute-done((bf16[32,3072]{1,0:T(8,128)(2,1)S(1)}, bf16[32,3072]{1,0:T(8,128)(2,1)S(1)}, u32[]{:S(2)}, u32[]{:S(2)}) %collective-permute-start.58) | collective-permute-done | bytes 196640 | tf_op jit(solution)/shard_map/ppermute | solution.py:28
  334.8 5.5 %collective-permute-done.59.refs_1_ = bf16[32,3072]{1,0:T(8,128)(2,1)S(1)} collective-permute-done((bf16[32,3072]{1,0:T(8,128)(2,1)S(1)}, bf16[32,3072]{1,0:T(8,128)(2,1)S(1)}, u32[]{:S(2)}, u32[]{:S(2)}) %collective-permute-start.59) | collective-permute-done | bytes 196640 | tf_op jit(solution)/shard_map/ppermute | solution.py:24
  343.4 5.8 %collective-permute-done.78.refs_18_ = bf16[4,256,384]{2,1,0:T(8,128)(2,1)S(1)} collective-permute-done((bf16[4,256,384]{2,1,0:T(8,128)(2,1)S(1)}, bf16[4,256,384]{2,1,0:T(8,128)(2,1)S(1)}, u32[]{:S(2)}, u32[]{:S(2)}) %collective-permute-start.78) | collective-permute-done | bytes 786464 | tf_op jit(solution)/shard_map/ppermute | solution.py:44
  355.1 11.0 %collective-permute-done.77.refs_17_ = bf16[4,256,384]{2,1,0:T(8,128)(2,1)S(1)} collective-permute-done((bf16[4,256,384]{2,1,0:T(8,128)(2,1)S(1)}, bf16[4,256,384]{2,1,0:T(8,128)(2,1)S(1)}, u32[]{:S(2)}, u32[]{:S(2)}) %collective-permute-start.77) | collective-permute-done | bytes 786464 | tf_op jit(solution)/shard_map/ppermute | solution.py:44
  369.8 10.4 %collective-permute-done.80.refs_19_ = bf16[4,256,384]{2,1,0:T(8,128)(2,1)S(1)} collective-permute-done((bf16[4,256,384]{2,1,0:T(8,128)(2,1)S(1)}, bf16[4,256,384]{2,1,0:T(8,128)(2,1)S(1)}, u32[]{:S(2)}, u32[]{:S(2)}) %collective-permute-start.80) | collective-permute-done | bytes 786464 | tf_op jit(solution)/shard_map/ppermute | solution.py:44
  381.6 8.4 %shard_map.76 = (bf16[4,32,3072]{2,1,0:T(8,128)(2,1)S(1)}, bf16[4,32,3072]{2,1,0:T(8,128)(2,1)S(1)}) custom-call(s32[16]{0:T(128)S(1)} %stack.212.ctl, bf16[32,3072]{1,0:T(8,128)(2,1)S(1)} %fusion.11.refs_0_, bf16[32,3072]{1,0:T(8,128)(2,1)S(1)} %collective-permute-done.59.refs_1_, bf16[32,3072]{1,0:T(8,128)(2,1)S(1)} %collective-permute-done.60.refs_2_, ...), custom_call_target="tpu_custom_call" | custom-call | flops 2415919104 | bytes 14155776 | tf_op jit(solution)/shard_map/pallas_call | solution.py:156
  398.6 13.5 %collective-permute-done.95.refs_8_ = bf16[4,256,384]{2,1,0:T(8,128)(2,1)S(1)} collective-permute-done((bf16[4,256,384]{2,1,0:T(8,128)(2,1)S(1)}, bf16[4,256,384]{2,1,0:T(8,128)(2,1)S(1)}, u32[]{:S(2)}, u32[]{:S(2)}) %collective-permute-start.95) | collective-permute-done | bytes 786464 | tf_op jit(solution)/shard_map/ppermute | solution.py:36
  416.7 15.9 %collective-permute-done.96.refs_9_ = bf16[4,256,384]{2,1,0:T(8,128)(2,1)S(1)} collective-permute-done((bf16[4,256,384]{2,1,0:T(8,128)(2,1)S(1)}, bf16[4,256,384]{2,1,0:T(8,128)(2,1)S(1)}, u32[]{:S(2)}, u32[]{:S(2)}) %collective-permute-start.96) | collective-permute-done | bytes 786464 | tf_op jit(solution)/shard_map/ppermute | solution.py:36
  463.3 8.1 %shard_map.77 = (bf16[4,32,3072]{2,1,0:T(8,128)(2,1)S(1)}, bf16[4,32,3072]{2,1,0:T(8,128)(2,1)S(1)}) custom-call(s32[16]{0:T(128)S(1)} %stack.212.ctl, bf16[32,3072]{1,0:T(8,128)(2,1)S(1)} %fusion.14.refs_0_, bf16[32,3072]{1,0:T(8,128)(2,1)S(1)} %collective-permute-done.88.refs_1_, bf16[32,3072]{1,0:T(8,128)(2,1)S(1)} %collective-permute-done.89.refs_2_, ...), custom_call_target="tpu_custom_call" | custom-call | flops 2415919104 | bytes 14155776 | tf_op jit(solution)/shard_map/pallas_call | solution.py:156
  483.0 4.2 collective-permute-done.110
  (365 shorter events, 196.5 us)
Async XLA Ops:
  4.8 24.4 %all-to-all-start = ((bf16[32,48,384]{2,1,0:T(8,128)(2,1)}), bf16[32,48,384]{2,1,0:T(8,128)(2,1)S(1)}, u32[]{:S(2)}, u32[]{:S(2)}) async-start(bf16[32,48,384]{2,1,0:T(8,128)(2,1)} %bitcast.214), calls=%async_computation | async-start | bytes 2359296 | tf_op jit(solution)/shard_map/all_to_all | solution.py:289
  66.3 35.0 %collective-permute-start.10 = (bf16[4,256,384]{2,1,0:T(8,128)(2,1)S(1)}, bf16[4,256,384]{2,1,0:T(8,128)(2,1)S(1)}, u32[]{:S(2)}, u32[]{:S(2)}) collective-permute-start(bf16[4,256,384]{2,1,0:T(8,128)(2,1)S(1)} %collective-permute-done.9.refs_7_), channel_id=1, source_target_pairs={{0,8},{8,16},{16,24},{24,32},{32,40},{40,48},{48,56},{56,0},{1,9},... | collective-permute-start | bytes 2359304 | tf_op jit(solution)/shard_map/ppermute | solution.py:36
  66.3 38.6 %collective-permute-start.13 = (bf16[4,256,384]{2,1,0:T(8,128)(2,1)S(1)}, bf16[4,256,384]{2,1,0:T(8,128)(2,1)S(1)}, u32[]{:S(2)}, u32[]{:S(2)}) collective-permute-start(bf16[4,256,384]{2,1,0:T(8,128)(2,1)S(1)} %collective-permute-done.12.refs_10_), channel_id=1, source_target_pairs={{0,56},{8,0},{16,8},{24,16},{32,24},{40,32},{48,40},{56,48},{1,57}... | collective-permute-start | bytes 2359304 | tf_op jit(solution)/shard_map/ppermute | solution.py:40
  73.7 24.4 %collective-permute-start.66 = (bf16[384,384]{1,0:T(8,128)(2,1)S(1)}, bf16[384,384]{1,0:T(8,128)(2,1)}, u32[]{:S(2)}, u32[]{:S(2)}) collective-permute-start(bf16[384,384]{1,0:T(8,128)(2,1)S(1)} %get-tuple-element.64), channel_id=1, source_target_pairs={{64,128},{128,64},{192,0},{0,192},{65,129},{129,65},{193,1},{1,193... | collective-permute-start | bytes 884744 | tf_op jit(solution)/shard_map/ppermute | solution.py:48
  101.3 44.7 %collective-permute-start.11 = (bf16[4,256,384]{2,1,0:T(8,128)(2,1)S(1)}, bf16[4,256,384]{2,1,0:T(8,128)(2,1)S(1)}, u32[]{:S(2)}, u32[]{:S(2)}) collective-permute-start(bf16[4,256,384]{2,1,0:T(8,128)(2,1)S(1)} %collective-permute-done.10.refs_8_), channel_id=1, source_target_pairs={{0,8},{8,16},{16,24},{24,32},{32,40},{40,48},{48,56},{56,0},{1,9},... | collective-permute-start | bytes 2359304 | tf_op jit(solution)/shard_map/ppermute | solution.py:36
  101.5 33.1 %collective-permute-start.41 = (bf16[768,384]{1,0:T(8,128)(2,1)S(1)}, bf16[768,384]{1,0:T(8,128)(2,1)S(1)}, u32[]{:S(2)}, u32[]{:S(2)}) collective-permute-start(bf16[768,384]{1,0:T(8,128)(2,1)S(1)} %pad_maximum_fusion.10), channel_id=1, source_target_pairs={{0,8},{8,16},{16,24},{24,32},{32,40},{40,48},{48,56},{56,0},{1,9},... | collective-permute-start | bytes 1769480 | tf_op jit(solution)/shard_map/ppermute | solution.py:36
  105.0 30.3 %collective-permute-start.44 = (bf16[768,384]{1,0:T(8,128)(2,1)S(1)}, bf16[768,384]{1,0:T(8,128)(2,1)S(1)}, u32[]{:S(2)}, u32[]{:S(2)}) collective-permute-start(bf16[768,384]{1,0:T(8,128)(2,1)S(1)} %pad_maximum_fusion.10), channel_id=1, source_target_pairs={{0,56},{8,0},{16,8},{24,16},{32,24},{40,32},{48,40},{56,48},{1,57}... | collective-permute-start | bytes 1769480 | tf_op jit(solution)/shard_map/ppermute | solution.py:40
  105.0 41.5 %collective-permute-start.14 = (bf16[4,256,384]{2,1,0:T(8,128)(2,1)S(1)}, bf16[4,256,384]{2,1,0:T(8,128)(2,1)S(1)}, u32[]{:S(2)}, u32[]{:S(2)}) collective-permute-start(bf16[4,256,384]{2,1,0:T(8,128)(2,1)S(1)} %collective-permute-done.13.refs_11_), channel_id=1, source_target_pairs={{0,56},{8,0},{16,8},{24,16},{32,24},{40,32},{48,40},{56,48},{1,57}... | collective-permute-start | bytes 2359304 | tf_op jit(solution)/shard_map/ppermute | solution.py:40
  106.8 25.7 %collective-permute-start.23 = (bf16[128,384]{1,0:T(8,128)(2,1)S(1)}, bf16[128,384]{1,0:T(8,128)(2,1)S(1)}, u32[]{:S(2)}, u32[]{:S(2)}) collective-permute-start(bf16[128,384]{1,0:T(8,128)(2,1)S(1)} %collective-permute-done.19), channel_id=1, source_target_pairs={{0,8},{8,16},{16,24},{24,32},{32,40},{40,48},{48,56},{56,0},{1,9},... | collective-permute-start | bytes 294920 | tf_op jit(solution)/shard_map/ppermute | solution.py:36
  134.7 24.8 %collective-permute-start.25 = (bf16[4,128,384]{2,1,0:T(8,128)(2,1)S(1)}, bf16[4,128,384]{2,1,0:T(8,128)(2,1)}, u32[]{:S(2)}, u32[]{:S(2)}) collective-permute-start(bf16[4,128,384]{2,1,0:T(8,128)(2,1)S(1)} %pad_maximum_fusion.15.refs_16_), channel_id=1, source_target_pairs={{0,64},{64,0},{128,192},{192,128},{1,65},{65,1},{129,193},{193,129... | collective-permute-start | bytes 1179656 | tf_op jit(solution)/shard_map/ppermute | solution.py:44
  135.3 25.5 %collective-permute-start.24 = (bf16[4,128,384]{2,1,0:T(8,128)(2,1)S(1)}, bf16[4,128,384]{2,1,0:T(8,128)(2,1)}, u32[]{:S(2)}, u32[]{:S(2)}) collective-permute-start(bf16[4,128,384]{2,1,0:T(8,128)(2,1)S(1)} %pad_maximum_fusion.14.refs_15_), channel_id=1, source_target_pairs={{0,64},{64,0},{128,192},{192,128},{1,65},{65,1},{129,193},{193,129... | collective-permute-start | bytes 1179656 | tf_op jit(solution)/shard_map/ppermute | solution.py:44
  165.4 28.5 %collective-permute-start.45 = (bf16[768,384]{1,0:T(8,128)(2,1)}, bf16[768,384]{1,0:T(8,128)(2,1)S(1)}, u32[]{:S(2)}, u32[]{:S(2)}) collective-permute-start(bf16[768,384]{1,0:T(8,128)(2,1)} %copy-done.25), channel_id=1, source_target_pairs={{0,56},{8,0},{16,8},{24,16},{32,24},{40,32},{48,40},{56,48},{1,57}... | collective-permute-start | bytes 1769480 | tf_op jit(solution)/shard_map/ppermute | solution.py:40
  169.5 58.1 %collective-permute-start.68 = (bf16[4,128,384]{2,1,0:T(8,128)(2,1)S(1)}, bf16[4,128,384]{2,1,0:T(8,128)(2,1)S(1)}, u32[]{:S(2)}, u32[]{:S(2)}) collective-permute-start(bf16[4,128,384]{2,1,0:T(8,128)(2,1)S(1)} %pad_maximum_fusion.13.refs_6_), channel_id=1, source_target_pairs={{0,8},{8,16},{16,24},{24,32},{32,40},{40,48},{48,56},{56,0},{1,9},... | collective-permute-start | bytes 1179656 | tf_op jit(solution)/shard_map/ppermute | solution.py:36
  202.5 34.3 %collective-permute-start.50 = (bf16[4,384,384]{2,1,0:T(8,128)(2,1)S(1)}, bf16[4,384,384]{2,1,0:T(8,128)(2,1)S(1)}, u32[]{:S(2)}, u32[]{:S(2)}) collective-permute-start(bf16[4,384,384]{2,1,0:T(8,128)(2,1)S(1)} %pad_maximum_fusion.refs_6_), channel_id=1, source_target_pairs={{64,128},{128,64},{192,0},{0,192},{65,129},{129,65},{193,1},{1,193... | collective-permute-start | bytes 3538952 | tf_op jit(solution)/shard_map/ppermute | solution.py:48
  210.9 28.9 %collective-permute-start.49 = (bf16[4,384,384]{2,1,0:T(8,128)(2,1)S(1)}, bf16[4,384,384]{2,1,0:T(8,128)(2,1)S(1)}, u32[]{:S(2)}, u32[]{:S(2)}) collective-permute-start(bf16[4,384,384]{2,1,0:T(8,128)(2,1)S(1)} %pad_maximum_fusion.1.refs_7_), channel_id=1, source_target_pairs={{0,64},{64,0},{128,192},{192,128},{1,65},{65,1},{129,193},{193,129... | collective-permute-start | bytes 3538952 | tf_op jit(solution)/shard_map/ppermute | solution.py:44
  227.7 37.5 %collective-permute-start.48 = (bf16[4,384,384]{2,1,0:T(8,128)(2,1)S(1)}, bf16[4,384,384]{2,1,0:T(8,128)(2,1)S(1)}, u32[]{:S(2)}, u32[]{:S(2)}) collective-permute-start(bf16[4,384,384]{2,1,0:T(8,128)(2,1)S(1)} %pad_maximum_fusion.refs_6_), channel_id=1, source_target_pairs={{0,64},{64,0},{128,192},{192,128},{1,65},{65,1},{129,193},{193,129... | collective-permute-start | bytes 3538952 | tf_op jit(solution)/shard_map/ppermute | solution.py:44
  234.6 30.5 %collective-permute-start.53 = (bf16[4,384,384]{2,1,0:T(8,128)(2,1)S(1)}, bf16[4,384,384]{2,1,0:T(8,128)(2,1)S(1)}, u32[]{:S(2)}, u32[]{:S(2)}) collective-permute-start(bf16[4,384,384]{2,1,0:T(8,128)(2,1)S(1)} %pad_maximum_fusion.1.refs_7_), channel_id=1, source_target_pairs={{64,128},{128,64},{192,0},{0,192},{65,129},{129,65},{193,1},{1,193... | collective-permute-start | bytes 3538952 | tf_op jit(solution)/shard_map/ppermute | solution.py:48
  236.7 52.1 %collective-permute-start.51 = (bf16[4,384,384]{2,1,0:T(8,128)(2,1)S(1)}, bf16[4,384,384]{2,1,0:T(8,128)(2,1)S(1)}, u32[]{:S(2)}, u32[]{:S(2)}) collective-permute-start(bf16[4,384,384]{2,1,0:T(8,128)(2,1)S(1)} %collective-permute-done.50.refs_12_), channel_id=1, source_target_pairs={{0,64},{64,0},{128,192},{192,128},{1,65},{65,1},{129,193},{193,129... | collective-permute-start | bytes 3538952 | tf_op jit(solution)/shard_map/ppermute | solution.py:44
  239.9 50.7 %collective-permute-start.52 = (bf16[4,384,384]{2,1,0:T(8,128)(2,1)S(1)}, bf16[4,384,384]{2,1,0:T(8,128)(2,1)S(1)}, u32[]{:S(2)}, u32[]{:S(2)}) collective-permute-start(bf16[4,384,384]{2,1,0:T(8,128)(2,1)S(1)} %collective-permute-done.49.refs_9_), channel_id=1, source_target_pairs={{64,128},{128,64},{192,0},{0,192},{65,129},{129,65},{193,1},{1,193... | collective-permute-start | bytes 3538952 | tf_op jit(solution)/shard_map/ppermute | solution.py:48
  248.7 41.9 %collective-permute-start.39 = (bf16[3,32,3072]{2,1,0:T(8,128)(2,1)S(1)}, bf16[3,32,3072]{2,1,0:T(8,128)(2,1)S(1)}, u32[]{:S(2)}, u32[]{:S(2)}) collective-permute-start(bf16[3,32,3072]{2,1,0:T(8,128)(2,1)S(1)} %pad_maximum_fusion.9), channel_id=1, source_target_pairs={{0,1},{1,0},{2,3},{3,2},{4,5},{5,4},{6,7},{7,6},{8,9},{9,8},{10,11... | collective-permute-start | bytes 1769480 | tf_op jit(solution)/shard_map/ppermute | solution.py:32
  265.1 25.4 %collective-permute-start.40 = (bf16[32,3072]{1,0:T(8,128)(2,1)S(1)}, bf16[32,3072]{1,0:T(8,128)(2,1)S(1)}, u32[]{:S(2)}, u32[]{:S(2)}) collective-permute-start(bf16[32,3072]{1,0:T(8,128)(2,1)S(1)} %constant_dynamic-update-slice_fusion.2.refs_3_), channel_id=1, source_target_pairs={{0,1},{1,0},{2,3},{3,2},{4,5},{5,4},{6,7},{7,6},{8,9},{9,8},{10,11... | collective-permute-start | bytes 589832 | tf_op jit(solution)/shard_map/ppermute | solution.py:32
  265.2 34.9 %collective-permute-start.69 = (bf16[4,128,384]{2,1,0:T(8,128)(2,1)S(1)}, bf16[4,128,384]{2,1,0:T(8,128)(2,1)S(1)}, u32[]{:S(2)}, u32[]{:S(2)}) collective-permute-start(bf16[4,128,384]{2,1,0:T(8,128)(2,1)S(1)} %collective-permute-done.68.refs_7_), channel_id=1, source_target_pairs={{0,8},{8,16},{16,24},{24,32},{32,40},{40,48},{48,56},{56,0},{1,9},... | collective-permute-start | bytes 1179656 | tf_op jit(solution)/shard_map/ppermute | solution.py:36
  300.1 30.4 %collective-permute-start.70 = (bf16[4,128,384]{2,1,0:T(8,128)(2,1)S(1)}, bf16[4,128,384]{2,1,0:T(8,128)(2,1)S(1)}, u32[]{:S(2)}, u32[]{:S(2)}) collective-permute-start(bf16[4,128,384]{2,1,0:T(8,128)(2,1)S(1)} %collective-permute-done.69.refs_8_), channel_id=1, source_target_pairs={{0,8},{8,16},{16,24},{24,32},{32,40},{40,48},{48,56},{56,0},{1,9},... | collective-permute-start | bytes 1179656 | tf_op jit(solution)/shard_map/ppermute | solution.py:36
  300.4 30.5 %collective-permute-start.73 = (bf16[4,128,384]{2,1,0:T(8,128)(2,1)S(1)}, bf16[4,128,384]{2,1,0:T(8,128)(2,1)S(1)}, u32[]{:S(2)}, u32[]{:S(2)}) collective-permute-start(bf16[4,128,384]{2,1,0:T(8,128)(2,1)S(1)} %collective-permute-done.72.refs_11_), channel_id=1, source_target_pairs={{0,56},{8,0},{16,8},{24,16},{32,24},{40,32},{48,40},{56,48},{1,57}... | collective-permute-start | bytes 1179656 | tf_op jit(solution)/shard_map/ppermute | solution.py:40
  309.7 33.5 %collective-permute-start.79 = (bf16[4,256,384]{2,1,0:T(8,128)(2,1)S(1)}, bf16[4,256,384]{2,1,0:T(8,128)(2,1)S(1)}, u32[]{:S(2)}, u32[]{:S(2)}) collective-permute-start(bf16[4,256,384]{2,1,0:T(8,128)(2,1)S(1)} %pad_maximum_fusion.6.refs_15_), channel_id=1, source_target_pairs={{64,128},{128,64},{192,0},{0,192},{65,129},{129,65},{193,1},{1,193... | collective-permute-start | bytes 2359304 | tf_op jit(solution)/shard_map/ppermute | solution.py:48
  340.3 25.8 %collective-permute-start.77 = (bf16[4,256,384]{2,1,0:T(8,128)(2,1)S(1)}, bf16[4,256,384]{2,1,0:T(8,128)(2,1)S(1)}, u32[]{:S(2)}, u32[]{:S(2)}) collective-permute-start(bf16[4,256,384]{2,1,0:T(8,128)(2,1)S(1)} %pad_maximum_fusion.6.refs_15_), channel_id=1, source_target_pairs={{0,64},{64,0},{128,192},{192,128},{1,65},{65,1},{129,193},{193,129... | collective-permute-start | bytes 2359304 | tf_op jit(solution)/shard_map/ppermute | solution.py:44
  341.8 24.5 %collective-permute-start.82 = (bf16[4,256,384]{2,1,0:T(8,128)(2,1)S(1)}, bf16[4,256,384]{2,1,0:T(8,128)(2,1)S(1)}, u32[]{:S(2)}, u32[]{:S(2)}) collective-permute-start(bf16[4,256,384]{2,1,0:T(8,128)(2,1)S(1)} %pad_maximum_fusion.7.refs_16_), channel_id=1, source_target_pairs={{64,128},{128,64},{192,0},{0,192},{65,129},{129,65},{193,1},{1,193... | collective-permute-start | bytes 2359304 | tf_op jit(solution)/shard_map/ppermute | solution.py:48
  343.2 37.0 %collective-permute-start.80 = (bf16[4,256,384]{2,1,0:T(8,128)(2,1)S(1)}, bf16[4,256,384]{2,1,0:T(8,128)(2,1)S(1)}, u32[]{:S(2)}, u32[]{:S(2)}) collective-permute-start(bf16[4,256,384]{2,1,0:T(8,128)(2,1)S(1)} %collective-permute-done.79.refs_21_), channel_id=1, source_target_pairs={{0,64},{64,0},{128,192},{192,128},{1,65},{65,1},{129,193},{193,129... | collective-permute-start | bytes 2359304 | tf_op jit(solution)/shard_map/ppermute | solution.py:44
  350.3 29.9 %collective-permute-start.81 = (bf16[4,256,384]{2,1,0:T(8,128)(2,1)S(1)}, bf16[4,256,384]{2,1,0:T(8,128)(2,1)S(1)}, u32[]{:S(2)}, u32[]{:S(2)}) collective-permute-start(bf16[4,256,384]{2,1,0:T(8,128)(2,1)S(1)} %collective-permute-done.78.refs_18_), channel_id=1, source_target_pairs={{64,128},{128,64},{192,0},{0,192},{65,129},{129,65},{193,1},{1,193... | collective-permute-start | bytes 2359304 | tf_op jit(solution)/shard_map/ppermute | solution.py:48
  355.1 26.6 %collective-permute-start.63 = (bf16[3,32,3072]{2,1,0:T(8,128)(2,1)S(1)}, bf16[3,32,3072]{2,1,0:T(8,128)(2,1)S(1)}, u32[]{:S(2)}, u32[]{:S(2)}) collective-permute-start(bf16[3,32,3072]{2,1,0:T(8,128)(2,1)S(1)} %pad_maximum_fusion.11), channel_id=1, source_target_pairs={{0,1},{1,0},{2,3},{3,2},{4,5},{5,4},{6,7},{7,6},{8,9},{9,8},{10,11... | collective-permute-start | bytes 1769480 | tf_op jit(solution)/shard_map/ppermute | solution.py:32
  366.2 24.5 %collective-permute-start.97 = (bf16[4,256,384]{2,1,0:T(8,128)(2,1)S(1)}, bf16[4,256,384]{2,1,0:T(8,128)(2,1)S(1)}, u32[]{:S(2)}, u32[]{:S(2)}) collective-permute-start(bf16[4,256,384]{2,1,0:T(8,128)(2,1)S(1)} %pad_maximum_fusion.2.refs_6_), channel_id=1, source_target_pairs={{0,56},{8,0},{16,8},{24,16},{32,24},{40,32},{48,40},{56,48},{1,57}... | collective-permute-start | bytes 2359304 | tf_op jit(solution)/shard_map/ppermute | solution.py:40
  394.2 42.2 %collective-permute-start.104 = (bf16[4,128,384]{2,1,0:T(8,128)(2,1)S(1)}, bf16[4,128,384]{2,1,0:T(8,128)(2,1)S(1)}, u32[]{:S(2)}, u32[]{:S(2)}) collective-permute-start(bf16[4,128,384]{2,1,0:T(8,128)(2,1)S(1)} %pad_maximum_fusion.16.refs_15_), channel_id=1, source_target_pairs={{64,128},{128,64},{192,0},{0,192},{65,129},{129,65},{193,1},{1,193... | collective-permute-start | bytes 1179656 | tf_op jit(solution)/shard_map/ppermute | solution.py:48
  (110 other events, 1610.4 us)
where the time goes:
time: 499 us; the launch traced here: 490 us
  waiting for transfers between devices  301 us (60%)
  starting transfers between devices  132 us (26%)
  Pallas kernels  37.5 us (8%)
  other arithmetic  9.43 us (2%)
  local copies, waits for them, and re-layouts  8.76 us (2%)
    ppermute x20, waiting for transfers between devices, up(): lax.ppermute(value, 'z', [(place, (place + 1) % 8) for place in range(8)])  100 us
    ppermute x16, waiting for transfers between devices, beside(): return lax.ppermute(value, 'pipe', NEAR)  88.6 us
    ppermute x19, starting transfers between devices, down(): lax.ppermute(value, 'z', [(place, (place - 1) % 8) for place in range(8)])  44.8 us
    ppermute x16, waiting for transfers between devices, far(): return lax.ppermute(value, 'y', FAR)  44.7 us
    pallas_call x4, Pallas kernels, run_block(): pl.pallas_call(functools.partial(block_kernel, tokens=tokens, shallow=sha...  34.9 us
    ppermute x14, starting transfers between devices, around(): return lax.ppermute(value, 'pipe', FAR)  28.9 us
    ppermute x16, starting transfers between devices, far(): return lax.ppermute(value, 'y', FAR)  26.1 us
    ppermute x19, waiting for transfers between devices, down(): lax.ppermute(value, 'z', [(place, (place - 1) % 8) for place in range(8)])  19.9 us
  transfers between devices with their start and end apart: 114, of which 48 were waited for; matrix products, arithmetic and copies ran while one was open for 3% of the time, Pallas kernels for 5%

commit v1 on v0

--- a/solution.py
+++ b/solution.py
@@ -77,8 +77,9 @@
         place = (depth + ctl[8 + slot]) & 7
         return pl.ds(pl.multiple_of(place * size, 128), size)
 
-    for slot in range(8):
-        cols, to = columns(slot), pl.ds(slot * size, size)
+    @pl.loop(0, 8)
+    def _(slot):
+        cols, to = columns(slot), pl.ds(pl.multiple_of(slot * size, 128), size)
         for block, (own, other) in enumerate(
             ((mine, swapped.at[0]), (by_near, swapped.at[1]), (cross, swapped_cross), (by_far, swapped.at[2]))
         ):
@@ -87,7 +88,9 @@
 
     for copy in copies:
         copy.wait()
-    for index in range(4):
+
+    @pl.loop(0, 4)
+    def _(index):
         array = section ^ index
 
         @pl.when(array != 3)
@@ -241,11 +244,12 @@
     return [four, *below, *above, up(below[-1][:2]), down(above[-1][2:])]
 
 
-def finish_across(lower, upper):
+def finish_across(lower, upper, later):
     by_beside = beside(lower), beside(upper)
     by_around = around(lower), around(upper)
-    crossed = beside(by_around[0]), around(by_beside[1])
-    return [lower, upper, *by_beside, *crossed, *by_around]
+    passed, later = lax.optimization_barrier((by_around[0], later))
+    crossed = beside(passed), around(by_beside[1])
+    return [lower, upper, *by_beside, *crossed, by_around[0], by_around[1]], later
 
 
 def spread(shards):
@@ -260,18 +264,27 @@
     below, above = deep(rest)
     lower = jnp.stack([rest, *below])
     upper = jnp.stack([*above, up(below[-1])])
-    across_all = [finish_across(lower, upper)]
+    across_all = [finish_across(lower, upper, ())[0]]
     rest = jnp.concatenate([one, two[cut[2] :], three[cut[3] :]])
     below, above = deep(rest)
     ends = up(below[-1][:size]), down(above[-1][size:])
     start = 0
+    stacks = []
     for layer in (1, 2, 3):
         stop = start + size - cut[layer]
         end = ends[0] if layer == 1 else ends[1][start - size : stop - size]
-        lower = jnp.stack([part[start:stop] for part in [rest, *below]])
-        upper = jnp.stack([part[start:stop] for part in above] + [end])
-        across_all.append(finish_across(lower, upper))
+        stacks.append(
+            (
+                jnp.stack([part[start:stop] for part in [rest, *below]]),
+                jnp.stack([part[start:stop] for part in above] + [end]),
+            )
+        )
         start = stop
+    lower, upper = stacks[0]
+    made, later = finish_across(lower, upper, stacks[1:])
+    across_all.append(made)
+    for layer, (lower, upper) in zip((2, 3), later):
+        across_all.append(finish_across(lower, upper, ())[0])
     return [early + late for early, late in zip(shallow, across_all)]
 
 

time: 499 us -> 498 us (level)
  the two profiles are of different devices: /device:TPU:6 before, /device:TPU:1 now
where the time goes in v1:
time: 498 us; the launch traced here: 489 us
  waiting for transfers between devices  263 us (53%)
  starting transfers between devices  176 us (35%)
  Pallas kernels  36.4 us (7%)
  other arithmetic  7.59 us (2%)
  local copies, waits for them, and re-layouts  5.22 us (1%)
    ppermute x20, waiting for transfers between devices, up(): lax.ppermute(value, 'z', [(place, (place + 1) % 8) for place in range(8)])  113 us
    ppermute x16, waiting for transfers between devices, beside(): return lax.ppermute(value, 'pipe', NEAR)  57.2 us
    ppermute x12, starting transfers between devices, swap(): return lax.ppermute(value, 'core', SWAP)  54.7 us
    ppermute x19, starting transfers between devices, down(): lax.ppermute(value, 'z', [(place, (place - 1) % 8) for place in range(8)])  38.1 us
    pallas_call x4, Pallas kernels, run_block(): pl.pallas_call(functools.partial(block_kernel, tokens=tokens, shallow=sha...  33.8 us
    ppermute x16, starting transfers between devices, far(): return lax.ppermute(value, 'y', FAR)  25.5 us
    ppermute x16, waiting for transfers between devices, far(): return lax.ppermute(value, 'y', FAR)  25.1 us
    ppermute x16, waiting for transfers between devices, near(): return lax.ppermute(value, 'y', NEAR)  21 us
  transfers between devices with their start and end apart: 114, of which 46 were waited for; matrix products, arithmetic and copies ran while one was open for 2% of the time, Pallas kernels for 6%

profile of v1, /device:TPU:1, one launch (start us, length us, event | category | flops | bytes accessed | tf_op | source)
XLA Modules:
  0.0 489.2 jit_solution(7747135105255326205)
XLA Ops:
  11.0 6.3 %all-to-all-start = ((bf16[32,48,384]{2,1,0:T(8,128)(2,1)}), bf16[32,48,384]{2,1,0:T(8,128)(2,1)S(1)}, u32[]{:S(2)}, u32[]{:S(2)}) async-start(bf16[32,48,384]{2,1,0:T(8,128)(2,1)} %bitcast.214), calls=%async_computation | async-start | bytes 2359296 | tf_op jit(solution)/shard_map/all_to_all | solution.py:302
  23.6 10.2 %collective-permute-done.2 = bf16[16,3072]{1,0:T(8,128)(2,1)S(1)} collective-permute-done((bf16[16,3072]{1,0:T(8,128)(2,1)S(1)}, bf16[16,3072]{1,0:T(8,128)(2,1)S(1)}, u32[]{:S(2)}, u32[]{:S(2)}) %collective-permute-start.2) | collective-permute-done | bytes 98336 | tf_op jit(solution)/shard_map/ppermute | solution.py:24
  49.6 9.2 %collective-permute-done.21 = bf16[128,384]{1,0:T(8,128)(2,1)S(1)} collective-permute-done((bf16[128,384]{1,0:T(8,128)(2,1)S(1)}, bf16[128,384]{1,0:T(8,128)(2,1)S(1)}, u32[]{:S(2)}, u32[]{:S(2)}) %collective-permute-start.21) | collective-permute-done | bytes 98336 | tf_op jit(solution)/shard_map/ppermute | solution.py:40
  66.1 8.9 %collective-permute-done.23 = bf16[128,384]{1,0:T(8,128)(2,1)S(1)} collective-permute-done((bf16[128,384]{1,0:T(8,128)(2,1)S(1)}, bf16[128,384]{1,0:T(8,128)(2,1)S(1)}, u32[]{:S(2)}, u32[]{:S(2)}) %collective-permute-start.23) | collective-permute-done | bytes 98336 | tf_op jit(solution)/shard_map/ppermute | solution.py:36
  77.6 7.1 %collective-permute-start.4 = (bf16[3,32,3072]{2,1,0:T(8,128)(2,1)S(1)}, bf16[3,32,3072]{2,1,0:T(8,128)(2,1)S(1)}, u32[]{:S(2)}, u32[]{:S(2)}) collective-permute-start(bf16[3,32,3072]{2,1,0:T(8,128)(2,1)S(1)} %pad_maximum_fusion.8), channel_id=1, source_target_pairs={{0,1},{1,0},{2,3},{3,2},{4,5},{5,4},{6,7},{7,6},{8,9},{9,8},{10,11... | collective-permute-start | bytes 1769480 | tf_op jit(solution)/shard_map/ppermute | solution.py:32
  84.7 7.1 %collective-permute-done.9.refs_7_ = bf16[4,256,384]{2,1,0:T(8,128)(2,1)S(1)} collective-permute-done((bf16[4,256,384]{2,1,0:T(8,128)(2,1)S(1)}, bf16[4,256,384]{2,1,0:T(8,128)(2,1)S(1)}, u32[]{:S(2)}, u32[]{:S(2)}) %collective-permute-start.9) | collective-permute-done | bytes 786464 | tf_op jit(solution)/shard_map/ppermute | solution.py:36
  94.5 6.6 %collective-permute-done.45 = bf16[768,384]{1,0:T(8,128)(2,1)S(1)} collective-permute-done((bf16[768,384]{1,0:T(8,128)(2,1)S(1)}, bf16[768,384]{1,0:T(8,128)(2,1)S(1)}, u32[]{:S(2)}, u32[]{:S(2)}) %collective-permute-start.45) | collective-permute-done | bytes 589856 | tf_op jit(solution)/shard_map/ppermute | solution.py:40
  104.5 16.7 %collective-permute-done.10.refs_8_ = bf16[4,256,384]{2,1,0:T(8,128)(2,1)S(1)} collective-permute-done((bf16[4,256,384]{2,1,0:T(8,128)(2,1)S(1)}, bf16[4,256,384]{2,1,0:T(8,128)(2,1)S(1)}, u32[]{:S(2)}, u32[]{:S(2)}) %collective-permute-start.10) | collective-permute-done | bytes 786464 | tf_op jit(solution)/shard_map/ppermute | solution.py:36
  124.1 9.8 %collective-permute-done.43 = bf16[768,384]{1,0:T(8,128)(2,1)S(1)} collective-permute-done((bf16[768,384]{1,0:T(8,128)(2,1)S(1)}, bf16[768,384]{1,0:T(8,128)(2,1)S(1)}, u32[]{:S(2)}, u32[]{:S(2)}) %collective-permute-start.43) | collective-permute-done | bytes 589856 | tf_op jit(solution)/shard_map/ppermute | solution.py:36
  135.6 15.2 %collective-permute-done.11.refs_9_ = bf16[4,256,384]{2,1,0:T(8,128)(2,1)S(1)} collective-permute-done((bf16[4,256,384]{2,1,0:T(8,128)(2,1)S(1)}, bf16[4,256,384]{2,1,0:T(8,128)(2,1)S(1)}, u32[]{:S(2)}, u32[]{:S(2)}) %collective-permute-start.11) | collective-permute-done | bytes 786464 | tf_op jit(solution)/shard_map/ppermute | solution.py:36
  156.1 9.0 %collective-permute-start.27 = (bf16[4,128,384]{2,1,0:T(8,128)(2,1)S(1)}, bf16[4,128,384]{2,1,0:T(8,128)(2,1)S(1)}, u32[]{:S(2)}, u32[]{:S(2)}) collective-permute-start(bf16[4,128,384]{2,1,0:T(8,128)(2,1)S(1)} %collective-permute-done.26.refs_21_), channel_id=1, source_target_pairs={{0,64},{64,0},{128,192},{192,128},{1,65},{65,1},{129,193},{193,129... | collective-permute-start | bytes 1179656 | tf_op jit(solution)/shard_map/ppermute | solution.py:44
  176.8 8.2 %shard_map.74 = (bf16[4,32,3072]{2,1,0:T(8,128)(2,1)S(1)}, bf16[4,32,3072]{2,1,0:T(8,128)(2,1)S(1)}) custom-call(s32[16]{0:T(128)S(1)} %stack.212.ctl, bf16[32,3072]{1,0:T(8,128)(2,1)S(1)} %fusion.4.refs_0_, bf16[32,3072]{1,0:T(8,128)(2,1)S(1)} %collective-permute-done.refs_1_, bf16[32,3072]{1,0:T(8,128)(2,1)S(1)} %collective-permute-done.1.refs_2_, ...), custom_call_target="tpu_custom_call" | custom-call | flops 2415919104 | bytes 14155776 | tf_op jit(solution)/shard_map/pallas_call | solution.py:159
  185.1 5.5 %collective-permute-start.30 = (bf16[4,32,3072]{2,1,0:T(8,128)(2,1)S(1)}, bf16[4,32,3072]{2,1,0:T(8,128)(2,1)S(1)}, u32[]{:S(2)}, u32[]{:S(2)}) collective-permute-start(bf16[4,32,3072]{2,1,0:T(8,128)(2,1)S(1)} %get-tuple-element.19), channel_id=1, source_target_pairs={{0,1},{1,0},{2,3},{3,2},{4,5},{5,4},{6,7},{7,6},{8,9},{9,8},{10,11... | collective-permute-start | bytes 2359304 | tf_op jit(solution)/shard_map/ppermute | solution.py:32
  193.9 6.6 %collective-permute-done.47 = bf16[384,384]{1,0:T(8,128)(2,1)S(1)} collective-permute-done((bf16[384,384]{1,0:T(8,128)(2,1)S(1)}, bf16[384,384]{1,0:T(8,128)(2,1)S(1)}, u32[]{:S(2)}, u32[]{:S(2)}) %collective-permute-start.47) | collective-permute-done | bytes 294944 | tf_op jit(solution)/shard_map/ppermute | solution.py:36
  219.7 14.2 %collective-permute-done.49.refs_9_ = bf16[4,384,384]{2,1,0:T(8,128)(2,1)S(1)} collective-permute-done((bf16[4,384,384]{2,1,0:T(8,128)(2,1)S(1)}, bf16[4,384,384]{2,1,0:T(8,128)(2,1)S(1)}, u32[]{:S(2)}, u32[]{:S(2)}) %collective-permute-start.49) | collective-permute-done | bytes 1179680 | tf_op jit(solution)/shard_map/ppermute | solution.py:44
  239.5 7.6 %collective-permute-start.39 = (bf16[3,32,3072]{2,1,0:T(8,128)(2,1)S(1)}, bf16[3,32,3072]{2,1,0:T(8,128)(2,1)S(1)}, u32[]{:S(2)}, u32[]{:S(2)}) collective-permute-start(bf16[3,32,3072]{2,1,0:T(8,128)(2,1)S(1)} %pad_maximum_fusion.9), channel_id=1, source_target_pairs={{0,1},{1,0},{2,3},{3,2},{4,5},{5,4},{6,7},{7,6},{8,9},{9,8},{10,11... | collective-permute-start | bytes 1769480 | tf_op jit(solution)/shard_map/ppermute | solution.py:32
  247.8 11.4 %collective-permute-done.52.refs_10_ = bf16[4,384,384]{2,1,0:T(8,128)(2,1)S(1)} collective-permute-done((bf16[4,384,384]{2,1,0:T(8,128)(2,1)S(1)}, bf16[4,384,384]{2,1,0:T(8,128)(2,1)S(1)}, u32[]{:S(2)}, u32[]{:S(2)}) %collective-permute-start.52) | collective-permute-done | bytes 1179680 | tf_op jit(solution)/shard_map/ppermute | solution.py:44
  259.9 6.2 %collective-permute-done.53.refs_11_ = bf16[4,384,384]{2,1,0:T(8,128)(2,1)S(1)} collective-permute-done((bf16[4,384,384]{2,1,0:T(8,128)(2,1)S(1)}, bf16[4,384,384]{2,1,0:T(8,128)(2,1)S(1)}, u32[]{:S(2)}, u32[]{:S(2)}) %collective-permute-start.53) | collective-permute-done | bytes 1179680 | tf_op jit(solution)/shard_map/ppermute | solution.py:48
  266.1 9.1 %shard_map.75 = (bf16[4,32,3072]{2,1,0:T(8,128)(2,1)S(1)}, bf16[4,32,3072]{2,1,0:T(8,128)(2,1)S(1)}) custom-call(s32[16]{0:T(128)S(1)} %stack.212.ctl, bf16[32,3072]{1,0:T(8,128)(2,1)S(1)} %fusion.8.refs_0_, bf16[32,3072]{1,0:T(8,128)(2,1)S(1)} %collective-permute-done.35.refs_1_, bf16[32,3072]{1,0:T(8,128)(2,1)S(1)} %collective-permute-done.36.refs_2_, ...), custom_call_target="tpu_custom_call" | custom-call | flops 2415919104 | bytes 14155776 | tf_op jit(solution)/shard_map/pallas_call | solution.py:159
  275.2 6.3 %collective-permute-start.55 = (bf16[4,32,3072]{2,1,0:T(8,128)(2,1)S(1)}, bf16[4,32,3072]{2,1,0:T(8,128)(2,1)S(1)}, u32[]{:S(2)}, u32[]{:S(2)}) collective-permute-start(bf16[4,32,3072]{2,1,0:T(8,128)(2,1)S(1)} %get-tuple-element.22), channel_id=1, source_target_pairs={{0,1},{1,0},{2,3},{3,2},{4,5},{5,4},{6,7},{7,6},{8,9},{9,8},{10,11... | collective-permute-start | bytes 2359304 | tf_op jit(solution)/shard_map/ppermute | solution.py:32
  284.3 9.2 %collective-permute-done.69.refs_7_ = bf16[4,128,384]{2,1,0:T(8,128)(2,1)S(1)} collective-permute-done((bf16[4,128,384]{2,1,0:T(8,128)(2,1)S(1)}, bf16[4,128,384]{2,1,0:T(8,128)(2,1)S(1)}, u32[]{:S(2)}, u32[]{:S(2)}) %collective-permute-start.69) | collective-permute-done | bytes 393248 | tf_op jit(solution)/shard_map/ppermute | solution.py:36
  298.4 6.0 %collective-permute-done.70.refs_8_ = bf16[4,128,384]{2,1,0:T(8,128)(2,1)S(1)} collective-permute-done((bf16[4,128,384]{2,1,0:T(8,128)(2,1)S(1)}, bf16[4,128,384]{2,1,0:T(8,128)(2,1)S(1)}, u32[]{:S(2)}, u32[]{:S(2)}) %collective-permute-start.70) | collective-permute-done | bytes 393248 | tf_op jit(solution)/shard_map/ppermute | solution.py:36
  317.5 7.7 %collective-permute-done.79.refs_21_ = bf16[4,256,384]{2,1,0:T(8,128)(2,1)S(1)} collective-permute-done((bf16[4,256,384]{2,1,0:T(8,128)(2,1)S(1)}, bf16[4,256,384]{2,1,0:T(8,128)(2,1)S(1)}, u32[]{:S(2)}, u32[]{:S(2)}) %collective-permute-start.79) | collective-permute-done | bytes 786464 | tf_op jit(solution)/shard_map/ppermute | solution.py:48
  342.6 7.6 %collective-permute-start.64 = (bf16[3,32,3072]{2,1,0:T(8,128)(2,1)S(1)}, bf16[3,32,3072]{2,1,0:T(8,128)(2,1)S(1)}, u32[]{:S(2)}, u32[]{:S(2)}) collective-permute-start(bf16[3,32,3072]{2,1,0:T(8,128)(2,1)S(1)} %pad_maximum_fusion.11), channel_id=1, source_target_pairs={{0,1},{1,0},{2,3},{3,2},{4,5},{5,4},{6,7},{7,6},{8,9},{9,8},{10,11... | collective-permute-start | bytes 1769480 | tf_op jit(solution)/shard_map/ppermute | solution.py:32
  350.3 7.7 %collective-permute-done.77.refs_17_ = bf16[4,256,384]{2,1,0:T(8,128)(2,1)S(1)} collective-permute-done((bf16[4,256,384]{2,1,0:T(8,128)(2,1)S(1)}, bf16[4,256,384]{2,1,0:T(8,128)(2,1)S(1)}, u32[]{:S(2)}, u32[]{:S(2)}) %collective-permute-start.77) | collective-permute-done | bytes 786464 | tf_op jit(solution)/shard_map/ppermute | solution.py:44
  357.9 7.6 %collective-permute-start.65 = (bf16[32,3072]{1,0:T(8,128)(2,1)S(1)}, bf16[32,3072]{1,0:T(8,128)(2,1)S(1)}, u32[]{:S(2)}, u32[]{:S(2)}) collective-permute-start(bf16[32,3072]{1,0:T(8,128)(2,1)S(1)} %constant_dynamic-update-slice_fusion.4.refs_3_), channel_id=1, source_target_pairs={{0,1},{1,0},{2,3},{3,2},{4,5},{5,4},{6,7},{7,6},{8,9},{9,8},{10,11... | collective-permute-start | bytes 589832 | tf_op jit(solution)/shard_map/ppermute | solution.py:32
  366.0 8.8 %collective-permute-done.80.refs_19_ = bf16[4,256,384]{2,1,0:T(8,128)(2,1)S(1)} collective-permute-done((bf16[4,256,384]{2,1,0:T(8,128)(2,1)S(1)}, bf16[4,256,384]{2,1,0:T(8,128)(2,1)S(1)}, u32[]{:S(2)}, u32[]{:S(2)}) %collective-permute-start.80) | collective-permute-done | bytes 786464 | tf_op jit(solution)/shard_map/ppermute | solution.py:44
  375.4 8.3 %shard_map.76 = (bf16[4,32,3072]{2,1,0:T(8,128)(2,1)S(1)}, bf16[4,32,3072]{2,1,0:T(8,128)(2,1)S(1)}) custom-call(s32[16]{0:T(128)S(1)} %stack.212.ctl, bf16[32,3072]{1,0:T(8,128)(2,1)S(1)} %fusion.11.refs_0_, bf16[32,3072]{1,0:T(8,128)(2,1)S(1)} %collective-permute-done.60.refs_1_, bf16[32,3072]{1,0:T(8,128)(2,1)S(1)} %collective-permute-done.61.refs_2_, ...), custom_call_target="tpu_custom_call" | custom-call | flops 2415919104 | bytes 14155776 | tf_op jit(solution)/shard_map/pallas_call | solution.py:159
  394.0 13.9 %collective-permute-done.95.refs_8_ = bf16[4,256,384]{2,1,0:T(8,128)(2,1)S(1)} collective-permute-done((bf16[4,256,384]{2,1,0:T(8,128)(2,1)S(1)}, bf16[4,256,384]{2,1,0:T(8,128)(2,1)S(1)}, u32[]{:S(2)}, u32[]{:S(2)}) %collective-permute-start.95) | collective-permute-done | bytes 786464 | tf_op jit(solution)/shard_map/ppermute | solution.py:36
  414.6 12.8 %collective-permute-done.96.refs_9_ = bf16[4,256,384]{2,1,0:T(8,128)(2,1)S(1)} collective-permute-done((bf16[4,256,384]{2,1,0:T(8,128)(2,1)S(1)}, bf16[4,256,384]{2,1,0:T(8,128)(2,1)S(1)}, u32[]{:S(2)}, u32[]{:S(2)}) %collective-permute-start.96) | collective-permute-done | bytes 786464 | tf_op jit(solution)/shard_map/ppermute | solution.py:36
  437.7 7.0 %collective-permute-done.103.refs_18_ = bf16[4,128,384]{2,1,0:T(8,128)(2,1)S(1)} collective-permute-done((bf16[4,128,384]{2,1,0:T(8,128)(2,1)S(1)}, bf16[4,128,384]{2,1,0:T(8,128)(2,1)S(1)}, u32[]{:S(2)}, u32[]{:S(2)}) %collective-permute-start.103) | collective-permute-done | bytes 393248 | tf_op jit(solution)/shard_map/ppermute | solution.py:44
  463.9 8.2 %shard_map.77 = (bf16[4,32,3072]{2,1,0:T(8,128)(2,1)S(1)}, bf16[4,32,3072]{2,1,0:T(8,128)(2,1)S(1)}) custom-call(s32[16]{0:T(128)S(1)} %stack.212.ctl, bf16[32,3072]{1,0:T(8,128)(2,1)S(1)} %fusion.14.refs_0_, bf16[32,3072]{1,0:T(8,128)(2,1)S(1)} %collective-permute-done.88.refs_1_, bf16[32,3072]{1,0:T(8,128)(2,1)S(1)} %collective-permute-done.89.refs_2_, ...), custom_call_target="tpu_custom_call" | custom-call | flops 2415919104 | bytes 14155776 | tf_op jit(solution)/shard_map/pallas_call | solution.py:159
  (311 shorter events, 201.7 us)
Async XLA Ops:
  11.0 24.7 %all-to-all-start = ((bf16[32,48,384]{2,1,0:T(8,128)(2,1)}), bf16[32,48,384]{2,1,0:T(8,128)(2,1)S(1)}, u32[]{:S(2)}, u32[]{:S(2)}) async-start(bf16[32,48,384]{2,1,0:T(8,128)(2,1)} %bitcast.214), calls=%async_computation | async-start | bytes 2359296 | tf_op jit(solution)/shard_map/all_to_all | solution.py:302
  21.6 23.0 %collective-permute-start.3 = (bf16[16,3072]{1,0:T(8,128)(2,1)S(1)}, bf16[16,3072]{1,0:T(8,128)(2,1)S(1)}, u32[]{:S(2)}, u32[]{:S(2)}) collective-permute-start(bf16[16,3072]{1,0:T(8,128)(2,1)S(1)} %slice.290), channel_id=1, source_target_pairs={{2,4},{4,2},{6,0},{0,6},{3,5},{5,3},{7,1},{1,7},{10,12},{12,10},{1... | collective-permute-start | bytes 294920 | tf_op jit(solution)/shard_map/ppermute | solution.py:28
  43.1 32.7 %collective-permute-start.44 = (bf16[768,384]{1,0:T(8,128)(2,1)S(1)}, bf16[768,384]{1,0:T(8,128)(2,1)S(1)}, u32[]{:S(2)}, u32[]{:S(2)}) collective-permute-start(bf16[768,384]{1,0:T(8,128)(2,1)S(1)} %pad_maximum_fusion.10), channel_id=1, source_target_pairs={{0,56},{8,0},{16,8},{24,16},{32,24},{40,32},{48,40},{56,48},{1,57}... | collective-permute-start | bytes 1769480 | tf_op jit(solution)/shard_map/ppermute | solution.py:40
  64.2 27.6 %collective-permute-start.9 = (bf16[4,256,384]{2,1,0:T(8,128)(2,1)S(1)}, bf16[4,256,384]{2,1,0:T(8,128)(2,1)S(1)}, u32[]{:S(2)}, u32[]{:S(2)}) collective-permute-start(bf16[4,256,384]{2,1,0:T(8,128)(2,1)S(1)} %pad_maximum_fusion.5.refs_6_), channel_id=1, source_target_pairs={{0,8},{8,16},{16,24},{24,32},{32,40},{40,48},{48,56},{56,0},{1,9},... | collective-permute-start | bytes 2359304 | tf_op jit(solution)/shard_map/ppermute | solution.py:36
  75.8 25.2 %collective-permute-start.45 = (bf16[768,384]{1,0:T(8,128)(2,1)S(1)}, bf16[768,384]{1,0:T(8,128)(2,1)S(1)}, u32[]{:S(2)}, u32[]{:S(2)}) collective-permute-start(bf16[768,384]{1,0:T(8,128)(2,1)S(1)} %collective-permute-done.44), channel_id=1, source_target_pairs={{0,56},{8,0},{16,8},{24,16},{32,24},{40,32},{48,40},{56,48},{1,57}... | collective-permute-start | bytes 1769480 | tf_op jit(solution)/shard_map/ppermute | solution.py:40
  76.0 28.5 %collective-permute-start.42 = (bf16[768,384]{1,0:T(8,128)(2,1)S(1)}, bf16[768,384]{1,0:T(8,128)(2,1)S(1)}, u32[]{:S(2)}, u32[]{:S(2)}) collective-permute-start(bf16[768,384]{1,0:T(8,128)(2,1)S(1)} %collective-permute-done.41), channel_id=1, source_target_pairs={{0,8},{8,16},{16,24},{24,32},{32,40},{40,48},{48,56},{56,0},{1,9},... | collective-permute-start | bytes 1769480 | tf_op jit(solution)/shard_map/ppermute | solution.py:36
  77.6 88.1 %collective-permute-start.4 = (bf16[3,32,3072]{2,1,0:T(8,128)(2,1)S(1)}, bf16[3,32,3072]{2,1,0:T(8,128)(2,1)S(1)}, u32[]{:S(2)}, u32[]{:S(2)}) collective-permute-start(bf16[3,32,3072]{2,1,0:T(8,128)(2,1)S(1)} %pad_maximum_fusion.8), channel_id=1, source_target_pairs={{0,1},{1,0},{2,3},{3,2},{4,5},{5,4},{6,7},{7,6},{8,9},{9,8},{10,11... | collective-permute-start | bytes 1769480 | tf_op jit(solution)/shard_map/ppermute | solution.py:32
  91.8 29.5 %collective-permute-start.10 = (bf16[4,256,384]{2,1,0:T(8,128)(2,1)S(1)}, bf16[4,256,384]{2,1,0:T(8,128)(2,1)S(1)}, u32[]{:S(2)}, u32[]{:S(2)}) collective-permute-start(bf16[4,256,384]{2,1,0:T(8,128)(2,1)S(1)} %collective-permute-done.9.refs_7_), channel_id=1, source_target_pairs={{0,8},{8,16},{16,24},{24,32},{32,40},{40,48},{48,56},{56,0},{1,9},... | collective-permute-start | bytes 2359304 | tf_op jit(solution)/shard_map/ppermute | solution.py:36
  91.8 29.5 %collective-permute-start.13 = (bf16[4,256,384]{2,1,0:T(8,128)(2,1)S(1)}, bf16[4,256,384]{2,1,0:T(8,128)(2,1)S(1)}, u32[]{:S(2)}, u32[]{:S(2)}) collective-permute-start(bf16[4,256,384]{2,1,0:T(8,128)(2,1)S(1)} %collective-permute-done.12.refs_10_), channel_id=1, source_target_pairs={{0,56},{8,0},{16,8},{24,16},{32,24},{40,32},{48,40},{56,48},{1,57}... | collective-permute-start | bytes 2359304 | tf_op jit(solution)/shard_map/ppermute | solution.py:40
  101.1 33.7 %collective-permute-start.46 = (bf16[768,384]{1,0:T(8,128)(2,1)S(1)}, bf16[768,384]{1,0:T(8,128)(2,1)S(1)}, u32[]{:S(2)}, u32[]{:S(2)}) collective-permute-start(bf16[768,384]{1,0:T(8,128)(2,1)S(1)} %collective-permute-done.45), channel_id=1, source_target_pairs={{0,56},{8,0},{16,8},{24,16},{32,24},{40,32},{48,40},{56,48},{1,57}... | collective-permute-start | bytes 1769480 | tf_op jit(solution)/shard_map/ppermute | solution.py:40
  104.4 29.5 %collective-permute-start.43 = (bf16[768,384]{1,0:T(8,128)(2,1)S(1)}, bf16[768,384]{1,0:T(8,128)(2,1)S(1)}, u32[]{:S(2)}, u32[]{:S(2)}) collective-permute-start(bf16[768,384]{1,0:T(8,128)(2,1)S(1)} %collective-permute-done.42), channel_id=1, source_target_pairs={{0,8},{8,16},{16,24},{24,32},{32,40},{40,48},{48,56},{56,0},{1,9},... | collective-permute-start | bytes 1769480 | tf_op jit(solution)/shard_map/ppermute | solution.py:36
  121.3 29.5 %collective-permute-start.11 = (bf16[4,256,384]{2,1,0:T(8,128)(2,1)S(1)}, bf16[4,256,384]{2,1,0:T(8,128)(2,1)S(1)}, u32[]{:S(2)}, u32[]{:S(2)}) collective-permute-start(bf16[4,256,384]{2,1,0:T(8,128)(2,1)S(1)} %collective-permute-done.10.refs_8_), channel_id=1, source_target_pairs={{0,8},{8,16},{16,24},{24,32},{32,40},{40,48},{48,56},{56,0},{1,9},... | collective-permute-start | bytes 2359304 | tf_op jit(solution)/shard_map/ppermute | solution.py:36
  121.3 32.5 %collective-permute-start.14 = (bf16[4,256,384]{2,1,0:T(8,128)(2,1)S(1)}, bf16[4,256,384]{2,1,0:T(8,128)(2,1)S(1)}, u32[]{:S(2)}, u32[]{:S(2)}) collective-permute-start(bf16[4,256,384]{2,1,0:T(8,128)(2,1)S(1)} %collective-permute-done.13.refs_11_), channel_id=1, source_target_pairs={{0,56},{8,0},{16,8},{24,16},{32,24},{40,32},{48,40},{56,48},{1,57}... | collective-permute-start | bytes 2359304 | tf_op jit(solution)/shard_map/ppermute | solution.py:40
  133.9 31.9 %collective-permute-start.24 = (bf16[4,128,384]{2,1,0:T(8,128)(2,1)S(1)}, bf16[4,128,384]{2,1,0:T(8,128)(2,1)S(1)}, u32[]{:S(2)}, u32[]{:S(2)}) collective-permute-start(bf16[4,128,384]{2,1,0:T(8,128)(2,1)S(1)} %pad_maximum_fusion.14.refs_15_), channel_id=1, source_target_pairs={{0,64},{64,0},{128,192},{192,128},{1,65},{65,1},{129,193},{193,129... | collective-permute-start | bytes 1179656 | tf_op jit(solution)/shard_map/ppermute | solution.py:44
  134.8 30.3 %collective-permute-start.25 = (bf16[4,128,384]{2,1,0:T(8,128)(2,1)S(1)}, bf16[4,128,384]{2,1,0:T(8,128)(2,1)S(1)}, u32[]{:S(2)}, u32[]{:S(2)}) collective-permute-start(bf16[4,128,384]{2,1,0:T(8,128)(2,1)S(1)} %pad_maximum_fusion.15.refs_16_), channel_id=1, source_target_pairs={{0,64},{64,0},{128,192},{192,128},{1,65},{65,1},{129,193},{193,129... | collective-permute-start | bytes 1179656 | tf_op jit(solution)/shard_map/ppermute | solution.py:44
  168.9 49.8 %collective-permute-start.67 = (bf16[384,384]{1,0:T(8,128)(2,1)S(1)}, bf16[384,384]{1,0:T(8,128)(2,1)S(1)}, u32[]{:S(2)}, u32[]{:S(2)}) collective-permute-start(bf16[384,384]{1,0:T(8,128)(2,1)S(1)} %get-tuple-element.70), channel_id=1, source_target_pairs={{64,128},{128,64},{192,0},{0,192},{65,129},{129,65},{193,1},{1,193... | collective-permute-start | bytes 884744 | tf_op jit(solution)/shard_map/ppermute | solution.py:48
  174.9 37.6 %collective-permute-start.50 = (bf16[4,384,384]{2,1,0:T(8,128)(2,1)S(1)}, bf16[4,384,384]{2,1,0:T(8,128)(2,1)S(1)}, u32[]{:S(2)}, u32[]{:S(2)}) collective-permute-start(bf16[4,384,384]{2,1,0:T(8,128)(2,1)S(1)} %pad_maximum_fusion.refs_6_), channel_id=1, source_target_pairs={{64,128},{128,64},{192,0},{0,192},{65,129},{129,65},{193,1},{1,193... | collective-permute-start | bytes 3538952 | tf_op jit(solution)/shard_map/ppermute | solution.py:48
  176.2 70.9 %collective-permute-start.48 = (bf16[4,384,384]{2,1,0:T(8,128)(2,1)S(1)}, bf16[4,384,384]{2,1,0:T(8,128)(2,1)S(1)}, u32[]{:S(2)}, u32[]{:S(2)}) collective-permute-start(bf16[4,384,384]{2,1,0:T(8,128)(2,1)S(1)} %pad_maximum_fusion.refs_6_), channel_id=1, source_target_pairs={{0,64},{64,0},{128,192},{192,128},{1,65},{65,1},{129,193},{193,129... | collective-permute-start | bytes 3538952 | tf_op jit(solution)/shard_map/ppermute | solution.py:44
  209.1 24.8 %collective-permute-start.49 = (bf16[4,384,384]{2,1,0:T(8,128)(2,1)S(1)}, bf16[4,384,384]{2,1,0:T(8,128)(2,1)S(1)}, u32[]{:S(2)}, u32[]{:S(2)}) collective-permute-start(bf16[4,384,384]{2,1,0:T(8,128)(2,1)S(1)} %pad_maximum_fusion.1.refs_7_), channel_id=1, source_target_pairs={{0,64},{64,0},{128,192},{192,128},{1,65},{65,1},{129,193},{193,129... | collective-permute-start | bytes 3538952 | tf_op jit(solution)/shard_map/ppermute | solution.py:44
  217.4 29.8 %collective-permute-start.54 = (bf16[4,384,384]{2,1,0:T(8,128)(2,1)S(1)}, bf16[4,384,384]{2,1,0:T(8,128)(2,1)S(1)}, u32[]{:S(2)}, u32[]{:S(2)}) collective-permute-start(bf16[4,384,384]{2,1,0:T(8,128)(2,1)S(1)} %pad_maximum_fusion.1.refs_7_), channel_id=1, source_target_pairs={{64,128},{128,64},{192,0},{0,192},{65,129},{129,65},{193,1},{1,193... | collective-permute-start | bytes 3538952 | tf_op jit(solution)/shard_map/ppermute | solution.py:48
  218.7 40.5 %collective-permute-start.52 = (bf16[4,384,384]{2,1,0:T(8,128)(2,1)S(1)}, bf16[4,384,384]{2,1,0:T(8,128)(2,1)S(1)}, u32[]{:S(2)}, u32[]{:S(2)}) collective-permute-start(bf16[4,384,384]{2,1,0:T(8,128)(2,1)S(1)} %collective-permute-done.50.refs_12_), channel_id=1, source_target_pairs={{0,64},{64,0},{128,192},{192,128},{1,65},{65,1},{129,193},{193,129... | collective-permute-start | bytes 3538952 | tf_op jit(solution)/shard_map/ppermute | solution.py:44
  234.0 32.2 %collective-permute-start.53 = (bf16[4,384,384]{2,1,0:T(8,128)(2,1)S(1)}, bf16[4,384,384]{2,1,0:T(8,128)(2,1)S(1)}, u32[]{:S(2)}, u32[]{:S(2)}) collective-permute-start(bf16[4,384,384]{2,1,0:T(8,128)(2,1)S(1)} %collective-permute-done.49.refs_9_), channel_id=1, source_target_pairs={{64,128},{128,64},{192,0},{0,192},{65,129},{129,65},{193,1},{1,193... | collective-permute-start | bytes 3538952 | tf_op jit(solution)/shard_map/ppermute | solution.py:48
  239.5 26.6 %collective-permute-start.39 = (bf16[3,32,3072]{2,1,0:T(8,128)(2,1)S(1)}, bf16[3,32,3072]{2,1,0:T(8,128)(2,1)S(1)}, u32[]{:S(2)}, u32[]{:S(2)}) collective-permute-start(bf16[3,32,3072]{2,1,0:T(8,128)(2,1)S(1)} %pad_maximum_fusion.9), channel_id=1, source_target_pairs={{0,1},{1,0},{2,3},{3,2},{4,5},{5,4},{6,7},{7,6},{8,9},{9,8},{10,11... | collective-permute-start | bytes 1769480 | tf_op jit(solution)/shard_map/ppermute | solution.py:32
  247.3 34.2 %collective-permute-start.66 = (bf16[384,384]{1,0:T(8,128)(2,1)S(1)}, bf16[384,384]{1,0:T(8,128)(2,1)S(1)}, u32[]{:S(2)}, u32[]{:S(2)}) collective-permute-start(bf16[384,384]{1,0:T(8,128)(2,1)S(1)} %get-tuple-element.70), channel_id=1, source_target_pairs={{0,64},{64,0},{128,192},{192,128},{1,65},{65,1},{129,193},{193,129... | collective-permute-start | bytes 884744 | tf_op jit(solution)/shard_map/ppermute | solution.py:44
  259.2 22.2 %collective-permute-start.68 = (bf16[384,384]{1,0:T(8,128)(2,1)S(1)}, bf16[384,384]{1,0:T(8,128)(2,1)S(1)}, u32[]{:S(2)}, u32[]{:S(2)}) collective-permute-start(bf16[384,384]{1,0:T(8,128)(2,1)S(1)} %collective-permute-done.67), channel_id=1, source_target_pairs={{0,64},{64,0},{128,192},{192,128},{1,65},{65,1},{129,193},{193,129... | collective-permute-start | bytes 884744 | tf_op jit(solution)/shard_map/ppermute | solution.py:44
  332.5 25.4 %collective-permute-start.77 = (bf16[4,256,384]{2,1,0:T(8,128)(2,1)S(1)}, bf16[4,256,384]{2,1,0:T(8,128)(2,1)S(1)}, u32[]{:S(2)}, u32[]{:S(2)}) collective-permute-start(bf16[4,256,384]{2,1,0:T(8,128)(2,1)S(1)} %pad_maximum_fusion.6.refs_15_), channel_id=1, source_target_pairs={{0,64},{64,0},{128,192},{192,128},{1,65},{65,1},{129,193},{193,129... | collective-permute-start | bytes 2359304 | tf_op jit(solution)/shard_map/ppermute | solution.py:44
  335.5 30.2 %collective-permute-start.82 = (bf16[4,256,384]{2,1,0:T(8,128)(2,1)S(1)}, bf16[4,256,384]{2,1,0:T(8,128)(2,1)S(1)}, u32[]{:S(2)}, u32[]{:S(2)}) collective-permute-start(bf16[4,256,384]{2,1,0:T(8,128)(2,1)S(1)} %pad_maximum_fusion.7.refs_16_), channel_id=1, source_target_pairs={{64,128},{128,64},{192,0},{0,192},{65,129},{129,65},{193,1},{1,193... | collective-permute-start | bytes 2359304 | tf_op jit(solution)/shard_map/ppermute | solution.py:48
  341.1 33.7 %collective-permute-start.80 = (bf16[4,256,384]{2,1,0:T(8,128)(2,1)S(1)}, bf16[4,256,384]{2,1,0:T(8,128)(2,1)S(1)}, u32[]{:S(2)}, u32[]{:S(2)}) collective-permute-start(bf16[4,256,384]{2,1,0:T(8,128)(2,1)S(1)} %collective-permute-done.79.refs_21_), channel_id=1, source_target_pairs={{0,64},{64,0},{128,192},{192,128},{1,65},{65,1},{129,193},{193,129... | collective-permute-start | bytes 2359304 | tf_op jit(solution)/shard_map/ppermute | solution.py:44
  341.4 34.0 %collective-permute-start.81 = (bf16[4,256,384]{2,1,0:T(8,128)(2,1)S(1)}, bf16[4,256,384]{2,1,0:T(8,128)(2,1)S(1)}, u32[]{:S(2)}, u32[]{:S(2)}) collective-permute-start(bf16[4,256,384]{2,1,0:T(8,128)(2,1)S(1)} %collective-permute-done.78.refs_18_), channel_id=1, source_target_pairs={{64,128},{128,64},{192,0},{0,192},{65,129},{129,65},{193,1},{1,193... | collective-permute-start | bytes 2359304 | tf_op jit(solution)/shard_map/ppermute | solution.py:48
  342.6 32.7 %collective-permute-start.64 = (bf16[3,32,3072]{2,1,0:T(8,128)(2,1)S(1)}, bf16[3,32,3072]{2,1,0:T(8,128)(2,1)S(1)}, u32[]{:S(2)}, u32[]{:S(2)}) collective-permute-start(bf16[3,32,3072]{2,1,0:T(8,128)(2,1)S(1)} %pad_maximum_fusion.11), channel_id=1, source_target_pairs={{0,1},{1,0},{2,3},{3,2},{4,5},{5,4},{6,7},{7,6},{8,9},{9,8},{10,11... | collective-permute-start | bytes 1769480 | tf_op jit(solution)/shard_map/ppermute | solution.py:32
  365.6 22.1 %collective-permute-start.94 = (bf16[4,256,384]{2,1,0:T(8,128)(2,1)S(1)}, bf16[4,256,384]{2,1,0:T(8,128)(2,1)S(1)}, u32[]{:S(2)}, u32[]{:S(2)}) collective-permute-start(bf16[4,256,384]{2,1,0:T(8,128)(2,1)S(1)} %pad_maximum_fusion.2.refs_6_), channel_id=1, source_target_pairs={{0,8},{8,16},{16,24},{24,32},{32,40},{40,48},{48,56},{56,0},{1,9},... | collective-permute-start | bytes 2359304 | tf_op jit(solution)/shard_map/ppermute | solution.py:36
  427.3 21.4 %collective-permute-start.102 = (bf16[4,128,384]{2,1,0:T(8,128)(2,1)S(1)}, bf16[4,128,384]{2,1,0:T(8,128)(2,1)S(1)}, u32[]{:S(2)}, u32[]{:S(2)}) collective-permute-start(bf16[4,128,384]{2,1,0:T(8,128)(2,1)S(1)} %pad_maximum_fusion.16.refs_15_), channel_id=1, source_target_pairs={{0,64},{64,0},{128,192},{192,128},{1,65},{65,1},{129,193},{193,129... | collective-permute-start | bytes 1179656 | tf_op jit(solution)/shard_map/ppermute | solution.py:44
  (83 other events, 1007.7 us)

commit v2 on v0

--- a/solution.py
+++ b/solution.py
@@ -57,38 +57,52 @@
     weights = refs[6 : 6 + pieces]
     keep, give, held, normed, sums, mixed_all, sems = refs[6 + pieces :]
     size = sums.shape[2]
-    places = []
-    if shallow:
-        rows = pl.ds(0, shallow)
-        places += [held.at[:, slot, rows] for slot in range(7)]
-        places += [held.at[0:2, 7, rows], held.at[2:4, 7, rows]]
-    if shallow < size:
-        rows = pl.ds(shallow, size - shallow)
-        places += [held.at[index // 2, pl.ds(index % 2 * 4, 4), rows] for index in range(8)]
-    copies = [
-        pltpu.make_async_copy(weights[index], place, sems.at[index])
-        for index, place in enumerate(places)
-    ]
-    for copy in copies:
-        copy.start()
+    copies = []
+    for index in range(4):
+        pairs = []
+        if shallow:
+            rows = pl.ds(0, shallow)
+            pairs += [(weights[slot].at[index], held.at[index, slot, rows]) for slot in range(7)]
+            pairs.append((weights[7 + index // 2].at[index % 2], held.at[index, 7, rows]))
+        if shallow < size:
+            rows = pl.ds(shallow, size - shallow)
+            base = 2 * index + (9 if shallow else 0)
+            pairs += [
+                (weights[base + half], held.at[index, pl.ds(4 * half, 4), rows]) for half in range(2)
+            ]
+        copies.append(
+            [
+                pltpu.make_async_copy(source, place, sems.at[index, number])
+                for number, (source, place) in enumerate(pairs)
+            ]
+        )
+    for group in copies:
+        for copy in group:
+            copy.start()
     flip, core, section, depth = ctl[0], ctl[1], ctl[4], ctl[5]
 
     def columns(slot):
         place = (depth + ctl[8 + slot]) & 7
         return pl.ds(pl.multiple_of(place * size, 128), size)
 
-    for slot in range(8):
-        cols, to = columns(slot), pl.ds(slot * size, size)
+    @pl.loop(0, 8)
+    def _(slot):
+        cols, to = columns(slot), pl.ds(pl.multiple_of(slot * size, 128), size)
         for block, (own, other) in enumerate(
             ((mine, swapped.at[0]), (by_near, swapped.at[1]), (cross, swapped_cross), (by_far, swapped.at[2]))
         ):
             normed[pl.ds(2 * block * tokens, tokens), to] = own[:, cols]
             normed[pl.ds((2 * block + 1) * tokens, tokens), to] = other[:, cols]
 
-    for copy in copies:
-        copy.wait()
-    for index in range(4):
+    @pl.loop(0, 4)
+    def _(index):
         array = section ^ index
+        for number, group in enumerate(copies):
+
+            @pl.when(index == number)
+            def _():
+                for copy in group:
+                    copy.wait()
 
         @pl.when(array != 3)
         def _():
@@ -165,7 +179,7 @@
             pltpu.VMEM((count, width), jnp.bfloat16),
             pltpu.VMEM((3, count, size), jnp.float32),
             pltpu.VMEM((count, size), jnp.bfloat16),
-            pltpu.SemaphoreType.DMA((17,)),
+            pltpu.SemaphoreType.DMA((4, 10)),
         ],
         compiler_params=pltpu.CompilerParams(vmem_limit_bytes=24 << 20),
         cost_estimate=pl.CostEstimate(

time: 499 us -> 519 us (1.040)
  Pallas kernels: 37.5 us -> 57.3 us
    pallas_call x4, Pallas kernels: 34.9 us -> 54.6 us  [run_block(): pl.pallas_call(functools.partial(block_kernel, tokens=tokens, shallow=sha...]
  transfers between devices with their start and end apart: 114 -> 114, of which waited for: 48 -> 47; matrix products, arithmetic and copies ran while one was open for 3% -> 3% of each run, Pallas kernels for 5% -> 7%
where the time goes in v2:
time: 519 us; the launch traced here: 510 us
  waiting for transfers between devices  299 us (58%)
  starting transfers between devices  134 us (26%)
  Pallas kernels  57.3 us (11%)
  other arithmetic  9.43 us (2%)
  local copies, waits for them, and re-layouts  8.76 us (2%)
    ppermute x20, waiting for transfers between devices, up(): lax.ppermute(value, 'z', [(place, (place + 1) % 8) for place in range(8)])  99.1 us
    ppermute x16, waiting for transfers between devices, beside(): return lax.ppermute(value, 'pipe', NEAR)  88.2 us
    pallas_call x4, Pallas kernels, run_block(): pl.pallas_call(functools.partial(block_kernel, tokens=tokens, shallow=sha...  54.6 us
    ppermute x19, starting transfers between devices, down(): lax.ppermute(value, 'z', [(place, (place - 1) % 8) for place in range(8)])  45 us
    ppermute x16, waiting for transfers between devices, far(): return lax.ppermute(value, 'y', FAR)  44.5 us
    ppermute x14, starting transfers between devices, around(): return lax.ppermute(value, 'pipe', FAR)  28.8 us
    ppermute x16, starting transfers between devices, far(): return lax.ppermute(value, 'y', FAR)  26.1 us
    ppermute x19, waiting for transfers between devices, down(): lax.ppermute(value, 'z', [(place, (place - 1) % 8) for place in range(8)])  19.8 us
  transfers between devices with their start and end apart: 114, of which 47 were waited for; matrix products, arithmetic and copies ran while one was open for 3% of the time, Pallas kernels for 7%

profile of v2, /device:TPU:6, one launch (start us, length us, event | category | flops | bytes accessed | tf_op | source)
XLA Modules:
  0.0 510.4 jit_solution(4099127502172053906)
XLA Ops:
  4.8 7.7 %all-to-all-start = ((bf16[32,48,384]{2,1,0:T(8,128)(2,1)}), bf16[32,48,384]{2,1,0:T(8,128)(2,1)S(1)}, u32[]{:S(2)}, u32[]{:S(2)}) async-start(bf16[32,48,384]{2,1,0:T(8,128)(2,1)} %bitcast.214), calls=%async_computation | async-start | bytes 2359296 | tf_op jit(solution)/shard_map/all_to_all | solution.py:303
  12.7 16.5 %all-to-all-done = bf16[32,48,384]{2,1,0:T(8,128)(2,1)S(1)} async-done(((bf16[32,48,384]{2,1,0:T(8,128)(2,1)}), bf16[32,48,384]{2,1,0:T(8,128)(2,1)S(1)}, u32[]{:S(2)}, u32[]{:S(2)}) %all-to-all-start) | async-done | bytes 1179680 | tf_op jit(solution)/shard_map/all_to_all | solution.py:303
  52.1 4.5 collective-permute-done.3
  56.7 9.6 %collective-permute-done.9.refs_7_ = bf16[4,256,384]{2,1,0:T(8,128)(2,1)S(1)} collective-permute-done((bf16[4,256,384]{2,1,0:T(8,128)(2,1)S(1)}, bf16[4,256,384]{2,1,0:T(8,128)(2,1)S(1)}, u32[]{:S(2)}, u32[]{:S(2)}) %collective-permute-start.9) | collective-permute-done | bytes 786464 | tf_op jit(solution)/shard_map/ppermute | solution.py:36
  75.9 11.4 %collective-permute-done.17 = bf16[128,384]{1,0:T(8,128)(2,1)S(1)} collective-permute-done((bf16[128,384]{1,0:T(8,128)(2,1)S(1)}, bf16[128,384]{1,0:T(8,128)(2,1)S(1)}, u32[]{:S(2)}, u32[]{:S(2)}) %collective-permute-start.17) | collective-permute-done | bytes 98336 | tf_op jit(solution)/shard_map/ppermute | solution.py:36
  89.3 4.2 collective-permute-done.18
  107.2 25.4 %collective-permute-done.23 = bf16[128,384]{1,0:T(8,128)(2,1)S(1)} collective-permute-done((bf16[128,384]{1,0:T(8,128)(2,1)S(1)}, bf16[128,384]{1,0:T(8,128)(2,1)S(1)}, u32[]{:S(2)}, u32[]{:S(2)}) %collective-permute-start.23) | collective-permute-done | bytes 98336 | tf_op jit(solution)/shard_map/ppermute | solution.py:36
  136.8 7.2 %collective-permute-done.26.refs_21_ = bf16[4,128,384]{2,1,0:T(8,128)(2,1)} collective-permute-done((bf16[4,128,384]{2,1,0:T(8,128)(2,1)S(1)}, bf16[4,128,384]{2,1,0:T(8,128)(2,1)}, u32[]{:S(2)}, u32[]{:S(2)}) %collective-permute-start.26) | collective-permute-done | bytes 393248 | tf_op jit(solution)/shard_map/ppermute | solution.py:48
  151.1 8.4 %collective-permute-done.67 = bf16[384,384]{1,0:T(8,128)(2,1)} collective-permute-done((bf16[384,384]{1,0:T(8,128)(2,1)}, bf16[384,384]{1,0:T(8,128)(2,1)}, u32[]{:S(2)}, u32[]{:S(2)}) %collective-permute-start.67) | collective-permute-done | bytes 294944 | tf_op jit(solution)/shard_map/ppermute | solution.py:44
  169.7 7.4 %collective-permute-done.42 = bf16[768,384]{1,0:T(8,128)(2,1)S(1)} collective-permute-done((bf16[768,384]{1,0:T(8,128)(2,1)}, bf16[768,384]{1,0:T(8,128)(2,1)S(1)}, u32[]{:S(2)}, u32[]{:S(2)}) %collective-permute-start.42) | collective-permute-done | bytes 589856 | tf_op jit(solution)/shard_map/ppermute | solution.py:36
  177.1 7.5 %collective-permute-done.15.refs_13_ = bf16[2,256,384]{2,1,0:T(8,128)(2,1)S(1)} collective-permute-done((bf16[2,256,384]{2,1,0:T(8,128)(2,1)S(1)}, bf16[2,256,384]{2,1,0:T(8,128)(2,1)S(1)}, u32[]{:S(2)}, u32[]{:S(2)}) %collective-permute-start.15) | collective-permute-done | bytes 393248 | tf_op jit(solution)/shard_map/ppermute | solution.py:36
  184.7 16.4 %shard_map.74 = (bf16[4,32,3072]{2,1,0:T(8,128)(2,1)S(1)}, bf16[4,32,3072]{2,1,0:T(8,128)(2,1)S(1)}) custom-call(s32[16]{0:T(128)S(1)} %stack.212.ctl, bf16[32,3072]{1,0:T(8,128)(2,1)S(1)} %copy-done.1, bf16[32,3072]{1,0:T(8,128)(2,1)S(1)} %collective-permute-done.refs_1_, bf16[32,3072]{1,0:T(8,128)(2,1)S(1)} %collective-permute-done.1.refs_2_, ...), custom_call_target="tpu_custom_call" | custom-call | flops 2415919104 | bytes 14155776 | tf_op jit(solution)/shard_map/pallas_call | solution.py:170
  205.6 4.2 collective-permute-done.31
  212.5 4.5 collective-permute-done.46
  220.2 4.5 collective-permute-done.34
  227.1 5.9 %collective-permute-done.36.refs_2_ = bf16[32,3072]{1,0:T(8,128)(2,1)S(1)} collective-permute-done((bf16[32,3072]{1,0:T(8,128)(2,1)S(1)}, bf16[32,3072]{1,0:T(8,128)(2,1)S(1)}, u32[]{:S(2)}, u32[]{:S(2)}) %collective-permute-start.36) | collective-permute-done | bytes 196640 | tf_op jit(solution)/shard_map/ppermute | solution.py:28
  236.3 5.6 %collective-permute-done.71.refs_10_ = bf16[4,128,384]{2,1,0:T(8,128)(2,1)S(1)} collective-permute-done((bf16[4,128,384]{2,1,0:T(8,128)(2,1)S(1)}, bf16[4,128,384]{2,1,0:T(8,128)(2,1)S(1)}, u32[]{:S(2)}, u32[]{:S(2)}) %collective-permute-start.71) | collective-permute-done | bytes 393248 | tf_op jit(solution)/shard_map/ppermute | solution.py:40
  251.3 5.1 %collective-permute-done.38 = bf16[16,3072]{1,0:T(8,128)(2,1)S(1)} collective-permute-done((bf16[16,3072]{1,0:T(8,128)(2,1)S(1)}, bf16[16,3072]{1,0:T(8,128)(2,1)S(1)}, u32[]{:S(2)}, u32[]{:S(2)}) %collective-permute-start.38) | collective-permute-done | bytes 98336 | tf_op jit(solution)/shard_map/ppermute | solution.py:28
  256.4 16.4 %collective-permute-done.48.refs_8_ = bf16[4,384,384]{2,1,0:T(8,128)(2,1)S(1)} collective-permute-done((bf16[4,384,384]{2,1,0:T(8,128)(2,1)S(1)}, bf16[4,384,384]{2,1,0:T(8,128)(2,1)S(1)}, u32[]{:S(2)}, u32[]{:S(2)}) %collective-permute-start.48) | collective-permute-done | bytes 1179680 | tf_op jit(solution)/shard_map/ppermute | solution.py:44
  273.0 23.5 %collective-permute-done.51.refs_10_ = bf16[4,384,384]{2,1,0:T(8,128)(2,1)S(1)} collective-permute-done((bf16[4,384,384]{2,1,0:T(8,128)(2,1)S(1)}, bf16[4,384,384]{2,1,0:T(8,128)(2,1)S(1)}, u32[]{:S(2)}, u32[]{:S(2)}) %collective-permute-start.51) | collective-permute-done | bytes 1179680 | tf_op jit(solution)/shard_map/ppermute | solution.py:44
  298.3 9.3 %shard_map.75 = (bf16[4,32,3072]{2,1,0:T(8,128)(2,1)S(1)}, bf16[4,32,3072]{2,1,0:T(8,128)(2,1)S(1)}) custom-call(s32[16]{0:T(128)S(1)} %stack.212.ctl, bf16[32,3072]{1,0:T(8,128)(2,1)S(1)} %fusion.8.refs_0_, bf16[32,3072]{1,0:T(8,128)(2,1)S(1)} %collective-permute-done.35.refs_1_, bf16[32,3072]{1,0:T(8,128)(2,1)S(1)} %collective-permute-done.36.refs_2_, ...), custom_call_target="tpu_custom_call" | custom-call | flops 2415919104 | bytes 14155776 | tf_op jit(solution)/shard_map/pallas_call | solution.py:170
  320.7 5.6 %collective-permute-done.76 = bf16[384,384]{1,0:T(8,128)(2,1)S(1)} collective-permute-done((bf16[384,384]{1,0:T(8,128)(2,1)S(1)}, bf16[384,384]{1,0:T(8,128)(2,1)S(1)}, u32[]{:S(2)}, u32[]{:S(2)}) %collective-permute-start.76) | collective-permute-done | bytes 294944 | tf_op jit(solution)/shard_map/ppermute | solution.py:40
  328.6 5.1 collective-permute-done.58
  342.4 5.5 %collective-permute-done.59.refs_1_ = bf16[32,3072]{1,0:T(8,128)(2,1)S(1)} collective-permute-done((bf16[32,3072]{1,0:T(8,128)(2,1)S(1)}, bf16[32,3072]{1,0:T(8,128)(2,1)S(1)}, u32[]{:S(2)}, u32[]{:S(2)}) %collective-permute-start.59) | collective-permute-done | bytes 196640 | tf_op jit(solution)/shard_map/ppermute | solution.py:24
  351.2 5.8 %collective-permute-done.78.refs_18_ = bf16[4,256,384]{2,1,0:T(8,128)(2,1)S(1)} collective-permute-done((bf16[4,256,384]{2,1,0:T(8,128)(2,1)S(1)}, bf16[4,256,384]{2,1,0:T(8,128)(2,1)S(1)}, u32[]{:S(2)}, u32[]{:S(2)}) %collective-permute-start.78) | collective-permute-done | bytes 786464 | tf_op jit(solution)/shard_map/ppermute | solution.py:44
  362.9 11.0 %collective-permute-done.77.refs_17_ = bf16[4,256,384]{2,1,0:T(8,128)(2,1)S(1)} collective-permute-done((bf16[4,256,384]{2,1,0:T(8,128)(2,1)S(1)}, bf16[4,256,384]{2,1,0:T(8,128)(2,1)S(1)}, u32[]{:S(2)}, u32[]{:S(2)}) %collective-permute-start.77) | collective-permute-done | bytes 786464 | tf_op jit(solution)/shard_map/ppermute | solution.py:44
  377.9 10.1 %collective-permute-done.80.refs_19_ = bf16[4,256,384]{2,1,0:T(8,128)(2,1)S(1)} collective-permute-done((bf16[4,256,384]{2,1,0:T(8,128)(2,1)S(1)}, bf16[4,256,384]{2,1,0:T(8,128)(2,1)S(1)}, u32[]{:S(2)}, u32[]{:S(2)}) %collective-permute-start.80) | collective-permute-done | bytes 786464 | tf_op jit(solution)/shard_map/ppermute | solution.py:44
  389.4 12.3 %shard_map.76 = (bf16[4,32,3072]{2,1,0:T(8,128)(2,1)S(1)}, bf16[4,32,3072]{2,1,0:T(8,128)(2,1)S(1)}) custom-call(s32[16]{0:T(128)S(1)} %stack.212.ctl, bf16[32,3072]{1,0:T(8,128)(2,1)S(1)} %fusion.11.refs_0_, bf16[32,3072]{1,0:T(8,128)(2,1)S(1)} %collective-permute-done.59.refs_1_, bf16[32,3072]{1,0:T(8,128)(2,1)S(1)} %collective-permute-done.60.refs_2_, ...), custom_call_target="tpu_custom_call" | custom-call | flops 2415919104 | bytes 14155776 | tf_op jit(solution)/shard_map/pallas_call | solution.py:170
  410.3 13.5 %collective-permute-done.95.refs_8_ = bf16[4,256,384]{2,1,0:T(8,128)(2,1)S(1)} collective-permute-done((bf16[4,256,384]{2,1,0:T(8,128)(2,1)S(1)}, bf16[4,256,384]{2,1,0:T(8,128)(2,1)S(1)}, u32[]{:S(2)}, u32[]{:S(2)}) %collective-permute-start.95) | collective-permute-done | bytes 786464 | tf_op jit(solution)/shard_map/ppermute | solution.py:36
  428.4 15.9 %collective-permute-done.96.refs_9_ = bf16[4,256,384]{2,1,0:T(8,128)(2,1)S(1)} collective-permute-done((bf16[4,256,384]{2,1,0:T(8,128)(2,1)S(1)}, bf16[4,256,384]{2,1,0:T(8,128)(2,1)S(1)}, u32[]{:S(2)}, u32[]{:S(2)}) %collective-permute-start.96) | collective-permute-done | bytes 786464 | tf_op jit(solution)/shard_map/ppermute | solution.py:36
  475.0 16.7 %shard_map.77 = (bf16[4,32,3072]{2,1,0:T(8,128)(2,1)S(1)}, bf16[4,32,3072]{2,1,0:T(8,128)(2,1)S(1)}) custom-call(s32[16]{0:T(128)S(1)} %stack.212.ctl, bf16[32,3072]{1,0:T(8,128)(2,1)S(1)} %fusion.14.refs_0_, bf16[32,3072]{1,0:T(8,128)(2,1)S(1)} %collective-permute-done.88.refs_1_, bf16[32,3072]{1,0:T(8,128)(2,1)S(1)} %collective-permute-done.89.refs_2_, ...), custom_call_target="tpu_custom_call" | custom-call | flops 2415919104 | bytes 14155776 | tf_op jit(solution)/shard_map/pallas_call | solution.py:170
  503.3 4.2 collective-permute-done.110
  (365 shorter events, 197.7 us)
Async XLA Ops:
  4.8 24.4 %all-to-all-start = ((bf16[32,48,384]{2,1,0:T(8,128)(2,1)}), bf16[32,48,384]{2,1,0:T(8,128)(2,1)S(1)}, u32[]{:S(2)}, u32[]{:S(2)}) async-start(bf16[32,48,384]{2,1,0:T(8,128)(2,1)} %bitcast.214), calls=%async_computation | async-start | bytes 2359296 | tf_op jit(solution)/shard_map/all_to_all | solution.py:303
  66.3 35.0 %collective-permute-start.10 = (bf16[4,256,384]{2,1,0:T(8,128)(2,1)S(1)}, bf16[4,256,384]{2,1,0:T(8,128)(2,1)S(1)}, u32[]{:S(2)}, u32[]{:S(2)}) collective-permute-start(bf16[4,256,384]{2,1,0:T(8,128)(2,1)S(1)} %collective-permute-done.9.refs_7_), channel_id=1, source_target_pairs={{0,8},{8,16},{16,24},{24,32},{32,40},{40,48},{48,56},{56,0},{1,9},... | collective-permute-start | bytes 2359304 | tf_op jit(solution)/shard_map/ppermute | solution.py:36
  66.3 38.6 %collective-permute-start.13 = (bf16[4,256,384]{2,1,0:T(8,128)(2,1)S(1)}, bf16[4,256,384]{2,1,0:T(8,128)(2,1)S(1)}, u32[]{:S(2)}, u32[]{:S(2)}) collective-permute-start(bf16[4,256,384]{2,1,0:T(8,128)(2,1)S(1)} %collective-permute-done.12.refs_10_), channel_id=1, source_target_pairs={{0,56},{8,0},{16,8},{24,16},{32,24},{40,32},{48,40},{56,48},{1,57}... | collective-permute-start | bytes 2359304 | tf_op jit(solution)/shard_map/ppermute | solution.py:40
  101.3 44.7 %collective-permute-start.11 = (bf16[4,256,384]{2,1,0:T(8,128)(2,1)S(1)}, bf16[4,256,384]{2,1,0:T(8,128)(2,1)S(1)}, u32[]{:S(2)}, u32[]{:S(2)}) collective-permute-start(bf16[4,256,384]{2,1,0:T(8,128)(2,1)S(1)} %collective-permute-done.10.refs_8_), channel_id=1, source_target_pairs={{0,8},{8,16},{16,24},{24,32},{32,40},{40,48},{48,56},{56,0},{1,9},... | collective-permute-start | bytes 2359304 | tf_op jit(solution)/shard_map/ppermute | solution.py:36
  101.5 33.1 %collective-permute-start.41 = (bf16[768,384]{1,0:T(8,128)(2,1)S(1)}, bf16[768,384]{1,0:T(8,128)(2,1)S(1)}, u32[]{:S(2)}, u32[]{:S(2)}) collective-permute-start(bf16[768,384]{1,0:T(8,128)(2,1)S(1)} %pad_maximum_fusion.10), channel_id=1, source_target_pairs={{0,8},{8,16},{16,24},{24,32},{32,40},{40,48},{48,56},{56,0},{1,9},... | collective-permute-start | bytes 1769480 | tf_op jit(solution)/shard_map/ppermute | solution.py:36
  105.0 30.3 %collective-permute-start.44 = (bf16[768,384]{1,0:T(8,128)(2,1)S(1)}, bf16[768,384]{1,0:T(8,128)(2,1)S(1)}, u32[]{:S(2)}, u32[]{:S(2)}) collective-permute-start(bf16[768,384]{1,0:T(8,128)(2,1)S(1)} %pad_maximum_fusion.10), channel_id=1, source_target_pairs={{0,56},{8,0},{16,8},{24,16},{32,24},{40,32},{48,40},{56,48},{1,57}... | collective-permute-start | bytes 1769480 | tf_op jit(solution)/shard_map/ppermute | solution.py:40
  105.0 41.5 %collective-permute-start.14 = (bf16[4,256,384]{2,1,0:T(8,128)(2,1)S(1)}, bf16[4,256,384]{2,1,0:T(8,128)(2,1)S(1)}, u32[]{:S(2)}, u32[]{:S(2)}) collective-permute-start(bf16[4,256,384]{2,1,0:T(8,128)(2,1)S(1)} %collective-permute-done.13.refs_11_), channel_id=1, source_target_pairs={{0,56},{8,0},{16,8},{24,16},{32,24},{40,32},{48,40},{56,48},{1,57}... | collective-permute-start | bytes 2359304 | tf_op jit(solution)/shard_map/ppermute | solution.py:40
  106.8 25.7 %collective-permute-start.23 = (bf16[128,384]{1,0:T(8,128)(2,1)S(1)}, bf16[128,384]{1,0:T(8,128)(2,1)S(1)}, u32[]{:S(2)}, u32[]{:S(2)}) collective-permute-start(bf16[128,384]{1,0:T(8,128)(2,1)S(1)} %collective-permute-done.19), channel_id=1, source_target_pairs={{0,8},{8,16},{16,24},{24,32},{32,40},{40,48},{48,56},{56,0},{1,9},... | collective-permute-start | bytes 294920 | tf_op jit(solution)/shard_map/ppermute | solution.py:36
  134.7 24.8 %collective-permute-start.25 = (bf16[4,128,384]{2,1,0:T(8,128)(2,1)S(1)}, bf16[4,128,384]{2,1,0:T(8,128)(2,1)}, u32[]{:S(2)}, u32[]{:S(2)}) collective-permute-start(bf16[4,128,384]{2,1,0:T(8,128)(2,1)S(1)} %pad_maximum_fusion.15.refs_16_), channel_id=1, source_target_pairs={{0,64},{64,0},{128,192},{192,128},{1,65},{65,1},{129,193},{193,129... | collective-permute-start | bytes 1179656 | tf_op jit(solution)/shard_map/ppermute | solution.py:44
  135.3 25.5 %collective-permute-start.24 = (bf16[4,128,384]{2,1,0:T(8,128)(2,1)S(1)}, bf16[4,128,384]{2,1,0:T(8,128)(2,1)}, u32[]{:S(2)}, u32[]{:S(2)}) collective-permute-start(bf16[4,128,384]{2,1,0:T(8,128)(2,1)S(1)} %pad_maximum_fusion.14.refs_15_), channel_id=1, source_target_pairs={{0,64},{64,0},{128,192},{192,128},{1,65},{65,1},{129,193},{193,129... | collective-permute-start | bytes 1179656 | tf_op jit(solution)/shard_map/ppermute | solution.py:44
  165.4 35.8 %collective-permute-start.45 = (bf16[768,384]{1,0:T(8,128)(2,1)}, bf16[768,384]{1,0:T(8,128)(2,1)S(1)}, u32[]{:S(2)}, u32[]{:S(2)}) collective-permute-start(bf16[768,384]{1,0:T(8,128)(2,1)} %copy-done.25), channel_id=1, source_target_pairs={{0,56},{8,0},{16,8},{24,16},{32,24},{40,32},{48,40},{56,48},{1,57}... | collective-permute-start | bytes 1769480 | tf_op jit(solution)/shard_map/ppermute | solution.py:40
  169.5 65.5 %collective-permute-start.68 = (bf16[4,128,384]{2,1,0:T(8,128)(2,1)S(1)}, bf16[4,128,384]{2,1,0:T(8,128)(2,1)S(1)}, u32[]{:S(2)}, u32[]{:S(2)}) collective-permute-start(bf16[4,128,384]{2,1,0:T(8,128)(2,1)S(1)} %pad_maximum_fusion.13.refs_6_), channel_id=1, source_target_pairs={{0,8},{8,16},{16,24},{24,32},{32,40},{40,48},{48,56},{56,0},{1,9},... | collective-permute-start | bytes 1179656 | tf_op jit(solution)/shard_map/ppermute | solution.py:36
  209.8 34.3 %collective-permute-start.50 = (bf16[4,384,384]{2,1,0:T(8,128)(2,1)S(1)}, bf16[4,384,384]{2,1,0:T(8,128)(2,1)S(1)}, u32[]{:S(2)}, u32[]{:S(2)}) collective-permute-start(bf16[4,384,384]{2,1,0:T(8,128)(2,1)S(1)} %pad_maximum_fusion.refs_6_), channel_id=1, source_target_pairs={{64,128},{128,64},{192,0},{0,192},{65,129},{129,65},{193,1},{1,193... | collective-permute-start | bytes 3538952 | tf_op jit(solution)/shard_map/ppermute | solution.py:48
  218.3 29.3 %collective-permute-start.49 = (bf16[4,384,384]{2,1,0:T(8,128)(2,1)S(1)}, bf16[4,384,384]{2,1,0:T(8,128)(2,1)S(1)}, u32[]{:S(2)}, u32[]{:S(2)}) collective-permute-start(bf16[4,384,384]{2,1,0:T(8,128)(2,1)S(1)} %pad_maximum_fusion.1.refs_7_), channel_id=1, source_target_pairs={{0,64},{64,0},{128,192},{192,128},{1,65},{65,1},{129,193},{193,129... | collective-permute-start | bytes 3538952 | tf_op jit(solution)/shard_map/ppermute | solution.py:44
  235.0 37.9 %collective-permute-start.48 = (bf16[4,384,384]{2,1,0:T(8,128)(2,1)S(1)}, bf16[4,384,384]{2,1,0:T(8,128)(2,1)S(1)}, u32[]{:S(2)}, u32[]{:S(2)}) collective-permute-start(bf16[4,384,384]{2,1,0:T(8,128)(2,1)S(1)} %pad_maximum_fusion.refs_6_), channel_id=1, source_target_pairs={{0,64},{64,0},{128,192},{192,128},{1,65},{65,1},{129,193},{193,129... | collective-permute-start | bytes 3538952 | tf_op jit(solution)/shard_map/ppermute | solution.py:44
  242.0 30.9 %collective-permute-start.53 = (bf16[4,384,384]{2,1,0:T(8,128)(2,1)S(1)}, bf16[4,384,384]{2,1,0:T(8,128)(2,1)S(1)}, u32[]{:S(2)}, u32[]{:S(2)}) collective-permute-start(bf16[4,384,384]{2,1,0:T(8,128)(2,1)S(1)} %pad_maximum_fusion.1.refs_7_), channel_id=1, source_target_pairs={{64,128},{128,64},{192,0},{0,192},{65,129},{129,65},{193,1},{1,193... | collective-permute-start | bytes 3538952 | tf_op jit(solution)/shard_map/ppermute | solution.py:48
  244.1 52.5 %collective-permute-start.51 = (bf16[4,384,384]{2,1,0:T(8,128)(2,1)S(1)}, bf16[4,384,384]{2,1,0:T(8,128)(2,1)S(1)}, u32[]{:S(2)}, u32[]{:S(2)}) collective-permute-start(bf16[4,384,384]{2,1,0:T(8,128)(2,1)S(1)} %collective-permute-done.50.refs_12_), channel_id=1, source_target_pairs={{0,64},{64,0},{128,192},{192,128},{1,65},{65,1},{129,193},{193,129... | collective-permute-start | bytes 3538952 | tf_op jit(solution)/shard_map/ppermute | solution.py:44
  247.6 50.7 %collective-permute-start.52 = (bf16[4,384,384]{2,1,0:T(8,128)(2,1)S(1)}, bf16[4,384,384]{2,1,0:T(8,128)(2,1)S(1)}, u32[]{:S(2)}, u32[]{:S(2)}) collective-permute-start(bf16[4,384,384]{2,1,0:T(8,128)(2,1)S(1)} %collective-permute-done.49.refs_9_), channel_id=1, source_target_pairs={{64,128},{128,64},{192,0},{0,192},{65,129},{129,65},{193,1},{1,193... | collective-permute-start | bytes 3538952 | tf_op jit(solution)/shard_map/ppermute | solution.py:48
  256.4 41.9 %collective-permute-start.39 = (bf16[3,32,3072]{2,1,0:T(8,128)(2,1)S(1)}, bf16[3,32,3072]{2,1,0:T(8,128)(2,1)S(1)}, u32[]{:S(2)}, u32[]{:S(2)}) collective-permute-start(bf16[3,32,3072]{2,1,0:T(8,128)(2,1)S(1)} %pad_maximum_fusion.9), channel_id=1, source_target_pairs={{0,1},{1,0},{2,3},{3,2},{4,5},{5,4},{6,7},{7,6},{8,9},{9,8},{10,11... | collective-permute-start | bytes 1769480 | tf_op jit(solution)/shard_map/ppermute | solution.py:32
  272.9 25.4 %collective-permute-start.40 = (bf16[32,3072]{1,0:T(8,128)(2,1)S(1)}, bf16[32,3072]{1,0:T(8,128)(2,1)S(1)}, u32[]{:S(2)}, u32[]{:S(2)}) collective-permute-start(bf16[32,3072]{1,0:T(8,128)(2,1)S(1)} %constant_dynamic-update-slice_fusion.2.refs_3_), channel_id=1, source_target_pairs={{0,1},{1,0},{2,3},{3,2},{4,5},{5,4},{6,7},{7,6},{8,9},{9,8},{10,11... | collective-permute-start | bytes 589832 | tf_op jit(solution)/shard_map/ppermute | solution.py:32
  272.9 34.8 %collective-permute-start.69 = (bf16[4,128,384]{2,1,0:T(8,128)(2,1)S(1)}, bf16[4,128,384]{2,1,0:T(8,128)(2,1)S(1)}, u32[]{:S(2)}, u32[]{:S(2)}) collective-permute-start(bf16[4,128,384]{2,1,0:T(8,128)(2,1)S(1)} %collective-permute-done.68.refs_7_), channel_id=1, source_target_pairs={{0,8},{8,16},{16,24},{24,32},{32,40},{40,48},{48,56},{56,0},{1,9},... | collective-permute-start | bytes 1179656 | tf_op jit(solution)/shard_map/ppermute | solution.py:36
  307.8 30.6 %collective-permute-start.70 = (bf16[4,128,384]{2,1,0:T(8,128)(2,1)S(1)}, bf16[4,128,384]{2,1,0:T(8,128)(2,1)S(1)}, u32[]{:S(2)}, u32[]{:S(2)}) collective-permute-start(bf16[4,128,384]{2,1,0:T(8,128)(2,1)S(1)} %collective-permute-done.69.refs_8_), channel_id=1, source_target_pairs={{0,8},{8,16},{16,24},{24,32},{32,40},{40,48},{48,56},{56,0},{1,9},... | collective-permute-start | bytes 1179656 | tf_op jit(solution)/shard_map/ppermute | solution.py:36
  308.1 30.5 %collective-permute-start.73 = (bf16[4,128,384]{2,1,0:T(8,128)(2,1)S(1)}, bf16[4,128,384]{2,1,0:T(8,128)(2,1)S(1)}, u32[]{:S(2)}, u32[]{:S(2)}) collective-permute-start(bf16[4,128,384]{2,1,0:T(8,128)(2,1)S(1)} %collective-permute-done.72.refs_11_), channel_id=1, source_target_pairs={{0,56},{8,0},{16,8},{24,16},{32,24},{40,32},{48,40},{56,48},{1,57}... | collective-permute-start | bytes 1179656 | tf_op jit(solution)/shard_map/ppermute | solution.py:40
  317.6 33.2 %collective-permute-start.79 = (bf16[4,256,384]{2,1,0:T(8,128)(2,1)S(1)}, bf16[4,256,384]{2,1,0:T(8,128)(2,1)S(1)}, u32[]{:S(2)}, u32[]{:S(2)}) collective-permute-start(bf16[4,256,384]{2,1,0:T(8,128)(2,1)S(1)} %pad_maximum_fusion.6.refs_15_), channel_id=1, source_target_pairs={{64,128},{128,64},{192,0},{0,192},{65,129},{129,65},{193,1},{1,193... | collective-permute-start | bytes 2359304 | tf_op jit(solution)/shard_map/ppermute | solution.py:48
  347.9 25.9 %collective-permute-start.77 = (bf16[4,256,384]{2,1,0:T(8,128)(2,1)S(1)}, bf16[4,256,384]{2,1,0:T(8,128)(2,1)S(1)}, u32[]{:S(2)}, u32[]{:S(2)}) collective-permute-start(bf16[4,256,384]{2,1,0:T(8,128)(2,1)S(1)} %pad_maximum_fusion.6.refs_15_), channel_id=1, source_target_pairs={{0,64},{64,0},{128,192},{192,128},{1,65},{65,1},{129,193},{193,129... | collective-permute-start | bytes 2359304 | tf_op jit(solution)/shard_map/ppermute | solution.py:44
  349.4 24.9 %collective-permute-start.82 = (bf16[4,256,384]{2,1,0:T(8,128)(2,1)S(1)}, bf16[4,256,384]{2,1,0:T(8,128)(2,1)S(1)}, u32[]{:S(2)}, u32[]{:S(2)}) collective-permute-start(bf16[4,256,384]{2,1,0:T(8,128)(2,1)S(1)} %pad_maximum_fusion.7.refs_16_), channel_id=1, source_target_pairs={{64,128},{128,64},{192,0},{0,192},{65,129},{129,65},{193,1},{1,193... | collective-permute-start | bytes 2359304 | tf_op jit(solution)/shard_map/ppermute | solution.py:48
  350.8 37.2 %collective-permute-start.80 = (bf16[4,256,384]{2,1,0:T(8,128)(2,1)S(1)}, bf16[4,256,384]{2,1,0:T(8,128)(2,1)S(1)}, u32[]{:S(2)}, u32[]{:S(2)}) collective-permute-start(bf16[4,256,384]{2,1,0:T(8,128)(2,1)S(1)} %collective-permute-done.79.refs_21_), channel_id=1, source_target_pairs={{0,64},{64,0},{128,192},{192,128},{1,65},{65,1},{129,193},{193,129... | collective-permute-start | bytes 2359304 | tf_op jit(solution)/shard_map/ppermute | solution.py:44
  358.1 29.9 %collective-permute-start.81 = (bf16[4,256,384]{2,1,0:T(8,128)(2,1)S(1)}, bf16[4,256,384]{2,1,0:T(8,128)(2,1)S(1)}, u32[]{:S(2)}, u32[]{:S(2)}) collective-permute-start(bf16[4,256,384]{2,1,0:T(8,128)(2,1)S(1)} %collective-permute-done.78.refs_18_), channel_id=1, source_target_pairs={{64,128},{128,64},{192,0},{0,192},{65,129},{129,65},{193,1},{1,193... | collective-permute-start | bytes 2359304 | tf_op jit(solution)/shard_map/ppermute | solution.py:48
  362.9 26.6 %collective-permute-start.63 = (bf16[3,32,3072]{2,1,0:T(8,128)(2,1)S(1)}, bf16[3,32,3072]{2,1,0:T(8,128)(2,1)S(1)}, u32[]{:S(2)}, u32[]{:S(2)}) collective-permute-start(bf16[3,32,3072]{2,1,0:T(8,128)(2,1)S(1)} %pad_maximum_fusion.11), channel_id=1, source_target_pairs={{0,1},{1,0},{2,3},{3,2},{4,5},{5,4},{6,7},{7,6},{8,9},{9,8},{10,11... | collective-permute-start | bytes 1769480 | tf_op jit(solution)/shard_map/ppermute | solution.py:32
  373.9 28.1 %collective-permute-start.94 = (bf16[4,256,384]{2,1,0:T(8,128)(2,1)S(1)}, bf16[4,256,384]{2,1,0:T(8,128)(2,1)S(1)}, u32[]{:S(2)}, u32[]{:S(2)}) collective-permute-start(bf16[4,256,384]{2,1,0:T(8,128)(2,1)S(1)} %pad_maximum_fusion.2.refs_6_), channel_id=1, source_target_pairs={{0,8},{8,16},{16,24},{24,32},{32,40},{40,48},{48,56},{56,0},{1,9},... | collective-permute-start | bytes 2359304 | tf_op jit(solution)/shard_map/ppermute | solution.py:36
  374.2 28.3 %collective-permute-start.97 = (bf16[4,256,384]{2,1,0:T(8,128)(2,1)S(1)}, bf16[4,256,384]{2,1,0:T(8,128)(2,1)S(1)}, u32[]{:S(2)}, u32[]{:S(2)}) collective-permute-start(bf16[4,256,384]{2,1,0:T(8,128)(2,1)S(1)} %pad_maximum_fusion.2.refs_6_), channel_id=1, source_target_pairs={{0,56},{8,0},{16,8},{24,16},{32,24},{40,32},{48,40},{56,48},{1,57}... | collective-permute-start | bytes 2359304 | tf_op jit(solution)/shard_map/ppermute | solution.py:40
  405.9 42.4 %collective-permute-start.104 = (bf16[4,128,384]{2,1,0:T(8,128)(2,1)S(1)}, bf16[4,128,384]{2,1,0:T(8,128)(2,1)S(1)}, u32[]{:S(2)}, u32[]{:S(2)}) collective-permute-start(bf16[4,128,384]{2,1,0:T(8,128)(2,1)S(1)} %pad_maximum_fusion.16.refs_15_), channel_id=1, source_target_pairs={{64,128},{128,64},{192,0},{0,192},{65,129},{129,65},{193,1},{1,193... | collective-permute-start | bytes 1179656 | tf_op jit(solution)/shard_map/ppermute | solution.py:48
  (110 other events, 1629.1 us)
